TPU v7x, 32 devices: a whole 2x2x4 slice. The times are simulated.
32 devices in a mesh: fsdp: 8 (over y, x, core), seq: 4 (over z).
Axes of the slice: x: 2, y: 2, z: 4, core: 2. Of those that a mesh axis runs over, the one named last changes fastest.
Arguments:
- tokens: bfloat16 [12288, 1024], P(('fsdp', 'seq')), may hold values from -6 to 6
- segment_ids: int32 [12288], P(('fsdp', 'seq')), may hold values from -1 to 1, as said below
- ln1_gain: bfloat16 [1024], P('fsdp'), may hold values from 0.099609375 to 1.8984375
- ln1_bias: bfloat16 [1024], P('fsdp'), may hold values from -3 to 3
- w_qkv: bfloat16 [1024, 3072], P('fsdp'), may hold values from -0.1875 to 0.1875
- q_bias: bfloat16 [1024], P('fsdp'), may hold values from -3 to 3
- v_bias: bfloat16 [1024], P('fsdp'), may hold values from -3 to 3
- w_out: bfloat16 [1024, 1024], P('fsdp'), may hold values from -0.75 to 0.75
- out_bias: bfloat16 [1024], P('fsdp'), may hold values from -3 to 3
- ln2_gain: bfloat16 [1024], P('fsdp'), may hold values from 0.099609375 to 1.8984375
- ln2_bias: bfloat16 [1024], P('fsdp'), may hold values from -3 to 3
- w_fc1: bfloat16 [1024, 4096], P('fsdp'), may hold values from -0.1875 to 0.1875
- fc1_bias: bfloat16 [4096], P('fsdp'), may hold values from -3 to 3
- w_fc2: bfloat16 [4096, 1024], P('fsdp'), may hold values from -0.09375 to 0.09375
- fc2_bias: bfloat16 [1024], P('fsdp'), may hold values from -3 to 3
- cotangent: bfloat16 [12288, 1024], P(('fsdp', 'seq')), may hold values from -6 to 6
Outputs:
- layer_output: bfloat16 [12288, 1024], P(('fsdp', 'seq'))
- tokens_grad: float32 [12288, 1024], P(('fsdp', 'seq'))
- ln1_gain_grad: float32 [1024], P(('fsdp', 'seq'))
- ln1_bias_grad: float32 [1024], P(('fsdp', 'seq'))
- w_qkv_grad: float32 [1024, 3072], P('fsdp', 'seq')
- q_bias_grad: float32 [1024], P(('fsdp', 'seq'))
- v_bias_grad: float32 [1024], P(('fsdp', 'seq'))
- w_out_grad: float32 [1024, 1024], P('fsdp', 'seq')
- out_bias_grad: float32 [1024], P(('fsdp', 'seq'))
- ln2_gain_grad: float32 [1024], P(('fsdp', 'seq'))
- ln2_bias_grad: float32 [1024], P(('fsdp', 'seq'))
- w_fc1_grad: float32 [1024, 4096], P('fsdp', 'seq')
- fc1_bias_grad: float32 [4096], P(('fsdp', 'seq'))
- w_fc2_grad: float32 [4096, 1024], P('fsdp', 'seq')
- fc2_bias_grad: float32 [1024], P(('fsdp', 'seq'))
Inputs may be any that keep to these rules, and one draw needn't show every extreme that they name: `segment_ids`: each span of 1536 slots (one index of fsdp) holds whole images of 577 slots from its first slot on, numbered 0, 1, 2, ... within the span, then padding slots marked -1; every span holds at least half of 2 images and some span holds 2.
All inputs are finite; a program needn't handle non-finite values.
Results may differ from a plain program's by a relative error of at most 0.019.
Values may be sent and summed in bfloat16 or wider, within the bound.
No kernel may reach another device: no remote copies, remote signals or barrier semaphores. Data moves between devices by JAX's collectives and lax.ppermute only.
A program may use at most 192 MiB of HBM per device.

v0:
```python
from functools import partial
import jax
import jax.numpy as jnp
from jax import lax
from jax.sharding import PartitionSpec as P

HD = 64
LEN = 577
norm_eps = 1e-06
masked_score = -1000000000.0


def normalize(values, gain, shift):
    row_mean = jnp.mean(values, axis=-1, keepdims=True)
    centered = values - row_mean
    variance = jnp.mean(centered * centered, axis=-1, keepdims=True)
    return centered * lax.rsqrt(variance + norm_eps) * gain + shift


def contract_rows(left, right):
    return lax.dot_general(
        left, right, (((0,), (0,)), ((), ())), preferred_element_type=jnp.float32
    )


def times_transposed(left, right):
    return lax.dot_general(
        left, right, (((1,), (1,)), ((), ())), preferred_element_type=jnp.float32
    )


def column_sum(values):
    return jnp.sum(values, axis=0, dtype=jnp.float32)


def shards_per_block(row_count, seq_count):
    for factor in range(1, seq_count + 1):
        if seq_count % factor == 0 and (row_count * factor >= 512 or factor == seq_count):
            return factor
    return seq_count


def add_window(total, delta, start):
    current = lax.dynamic_slice_in_dim(total, start, delta.shape[0], 0)
    return lax.dynamic_update_slice_in_dim(total, current + delta, start, 0)


def shards(
    tokens,
    segment_ids,
    ln1_gain,
    ln1_bias,
    w_qkv,
    q_bias,
    v_bias,
    w_out,
    out_bias,
    ln2_gain,
    ln2_bias,
    w_fc1,
    fc1_bias,
    w_fc2,
    fc2_bias,
    cotangent,
):
    row_count = tokens.shape[0]
    feature_width = tokens.shape[1]
    seq_count = lax.axis_size("seq")
    span_rows = row_count * seq_count
    local_heads = feature_width // seq_count // HD
    block_rows = row_count * shards_per_block(row_count, seq_count)
    block_count = span_rows // block_rows
    margin = LEN - 1
    window = block_rows + 2 * margin
    offsets = jnp.arange(block_count, dtype=jnp.int32) * block_rows
    scale = HD ** (-0.5)
    as_float = jnp.float32

    def weight_grad(left, right):
        return contract_rows(left, right)

    attn_set = (
        lax.all_gather(ln1_gain, "fsdp", axis=0, tiled=True),
        lax.all_gather(ln1_bias, "fsdp", axis=0, tiled=True),
        lax.all_gather(w_qkv, "fsdp", axis=0, tiled=True),
        lax.all_gather(q_bias, "fsdp", axis=0, tiled=True),
        lax.all_gather(v_bias, "fsdp", axis=0, tiled=True),
        lax.all_gather(w_out, "fsdp", axis=0, tiled=True),
        lax.all_gather(out_bias, "fsdp", axis=0, tiled=True),
    )
    span_labels = lax.all_gather(segment_ids, "seq", axis=0, tiled=True)
    inputs = tokens.astype(as_float)
    gain_one = attn_set[0].astype(as_float)
    shift_one = attn_set[1].astype(as_float)
    first_norm = normalize(inputs, gain_one, shift_one).astype(jnp.bfloat16)
    projected = jnp.dot(first_norm, attn_set[2], preferred_element_type=as_float)
    bias_all = jnp.concatenate(
        [
            attn_set[3].astype(as_float),
            jnp.zeros((feature_width,), as_float),
            attn_set[4].astype(as_float),
        ]
    )
    packed = (projected + bias_all).astype(jnp.bfloat16).reshape(row_count, 3, feature_width)
    head_rows = lax.all_to_all(packed, "seq", split_axis=2, concat_axis=0, tiled=True)
    query_heads = head_rows[:, 0, :].reshape(span_rows, local_heads, HD)
    key_heads = head_rows[:, 1, :].reshape(span_rows, local_heads, HD)
    value_heads = head_rows[:, 2, :].reshape(span_rows, local_heads, HD)
    key_padded = jnp.pad(key_heads, ((margin, margin), (0, 0), (0, 0)))
    value_padded = jnp.pad(value_heads, ((margin, margin), (0, 0), (0, 0)))
    label_padded = jnp.pad(span_labels, (margin, margin), constant_values=-2)

    def block_scores(offset):
        query_block = lax.dynamic_slice_in_dim(query_heads, offset, block_rows, 0)
        label_block = lax.dynamic_slice_in_dim(span_labels, offset, block_rows, 0)
        key_window = lax.dynamic_slice_in_dim(key_padded, offset, window, 0)
        value_window = lax.dynamic_slice_in_dim(value_padded, offset, window, 0)
        label_window = lax.dynamic_slice_in_dim(label_padded, offset, window, 0)
        scaled = (
            jnp.einsum("qhd,khd->hqk", query_block, key_window, preferred_element_type=as_float)
            * scale
        )
        same_image = label_block[:, None] == label_window[None, :]
        return (
            query_block,
            key_window,
            value_window,
            jnp.where(same_image[None], scaled, masked_score),
        )

    def block_forward(offset):
        unused_query, unused_key, value_window, scores = block_scores(offset)
        row_peak = jnp.max(scores, axis=-1, keepdims=True)
        lifted = jnp.exp(scores - row_peak)
        row_total = jnp.sum(lifted, axis=-1, keepdims=True)
        attn_probs = (lifted / row_total).astype(jnp.bfloat16)
        block_out = jnp.einsum(
            "hqk,khd->qhd", attn_probs, value_window, preferred_element_type=as_float
        ).astype(jnp.bfloat16)
        return (block_out, (row_peak + jnp.log(row_total))[..., 0])

    head_out, log_totals = lax.map(block_forward, offsets)
    head_flat = head_out.reshape(span_rows, local_heads * HD)
    attended = lax.all_to_all(head_flat, "seq", split_axis=0, concat_axis=1, tiled=True)
    mixed = jnp.dot(attended, attn_set[5], preferred_element_type=as_float) + attn_set[6].astype(
        as_float
    )
    middle = inputs + mixed
    mlp_set = (
        lax.all_gather(ln2_gain, "fsdp", axis=0, tiled=True),
        lax.all_gather(ln2_bias, "fsdp", axis=0, tiled=True),
        lax.all_gather(w_fc1, "fsdp", axis=0, tiled=True),
        lax.all_gather(fc1_bias, "fsdp", axis=0, tiled=True),
        lax.all_gather(w_fc2, "fsdp", axis=0, tiled=True),
        lax.all_gather(fc2_bias, "fsdp", axis=0, tiled=True),
    )
    gain_two = mlp_set[0].astype(as_float)
    shift_two = mlp_set[1].astype(as_float)
    second_norm = normalize(middle, gain_two, shift_two).astype(jnp.bfloat16)
    hidden = jnp.dot(second_norm, mlp_set[2], preferred_element_type=as_float) + mlp_set[3].astype(
        as_float
    )
    activated = jax.nn.gelu(hidden, approximate=False).astype(jnp.bfloat16)
    branch = jnp.dot(activated, mlp_set[4], preferred_element_type=as_float) + mlp_set[5].astype(
        as_float
    )
    valid = (segment_ids >= 0).astype(as_float)[:, None]
    layer_output = (valid * (middle + branch)).astype(jnp.bfloat16)
    grad_out = valid * cotangent.astype(as_float)
    grad_branch = grad_out.astype(jnp.bfloat16)
    fc2_bias_part = column_sum(grad_branch)
    w_fc2_part = weight_grad(activated, grad_branch)
    grad_act = times_transposed(grad_branch, mlp_set[4])
    unused_hidden, gelu_back = jax.vjp(partial(jax.nn.gelu, approximate=False), hidden)
    grad_hidden = gelu_back(grad_act)[0].astype(jnp.bfloat16)
    fc1_bias_part = column_sum(grad_hidden)
    w_fc1_part = weight_grad(second_norm, grad_hidden)
    grad_norm_two = times_transposed(grad_hidden, mlp_set[2])
    unused_two, norm_two_back = jax.vjp(
        normalize, middle, mlp_set[0].astype(as_float), mlp_set[1].astype(as_float)
    )
    grad_mid_norm, ln2_gain_part, ln2_bias_part = norm_two_back(grad_norm_two)
    grad_middle = grad_out + grad_mid_norm
    grad_mixed = grad_middle.astype(jnp.bfloat16)
    out_bias_part = column_sum(grad_mixed)
    w_out_part = weight_grad(attended, grad_mixed)
    grad_attended = times_transposed(grad_mixed, attn_set[5]).astype(jnp.bfloat16)
    grad_heads = lax.all_to_all(
        grad_attended, "seq", split_axis=1, concat_axis=0, tiled=True
    ).reshape(span_rows, local_heads, HD)

    def block_backward(running, inputs_block):
        key_total, value_total = running
        offset, log_block = inputs_block
        query_block, key_window, value_window, scores = block_scores(offset)
        grad_block = lax.dynamic_slice_in_dim(grad_heads, offset, block_rows, 0)
        probs_full = jnp.exp(scores - log_block[..., None])
        attn_probs = probs_full.astype(jnp.bfloat16)
        value_delta = jnp.einsum(
            "hqk,qhd->khd", attn_probs, grad_block, preferred_element_type=as_float
        )
        grad_probs = jnp.einsum(
            "qhd,khd->hqk", grad_block, value_window, preferred_element_type=as_float
        )
        row_inner = jnp.sum(grad_probs * probs_full, axis=-1, keepdims=True)
        grad_scores = (probs_full * (grad_probs - row_inner)).astype(jnp.bfloat16)
        grad_query = (
            jnp.einsum("hqk,khd->qhd", grad_scores, key_window, preferred_element_type=as_float)
            * scale
        )
        key_delta = (
            jnp.einsum("hqk,qhd->khd", grad_scores, query_block, preferred_element_type=as_float)
            * scale
        )
        return (
            (
                add_window(key_total, key_delta, offset),
                add_window(value_total, value_delta, offset),
            ),
            grad_query,
        )

    zero_heads = jnp.zeros((span_rows + 2 * margin, local_heads, HD), as_float)
    (key_padded_grad, value_padded_grad), query_grad = lax.scan(
        block_backward, (zero_heads, zero_heads), (offsets, log_totals)
    )
    key_grad = key_padded_grad[margin : margin + span_rows]
    value_grad = value_padded_grad[margin : margin + span_rows]
    head_grads = jnp.concatenate(
        [
            query_grad.reshape(span_rows, 1, local_heads * HD),
            key_grad.reshape(span_rows, 1, local_heads * HD),
            value_grad.reshape(span_rows, 1, local_heads * HD),
        ],
        axis=1,
    ).astype(jnp.bfloat16)
    token_grads = lax.all_to_all(
        head_grads, "seq", split_axis=0, concat_axis=2, tiled=True
    ).reshape(row_count, 3 * feature_width)
    q_bias_part = column_sum(token_grads[:, :feature_width])
    v_bias_part = column_sum(token_grads[:, 2 * feature_width :])
    w_qkv_part = weight_grad(first_norm, token_grads)
    grad_norm_one = times_transposed(token_grads, attn_set[2])
    unused_one, norm_one_back = jax.vjp(
        normalize, inputs, attn_set[0].astype(as_float), attn_set[1].astype(as_float)
    )
    grad_input_norm, ln1_gain_part, ln1_bias_part = norm_one_back(grad_norm_one)
    tokens_grad = grad_middle + grad_input_norm
    partial_sums = (
        lax.psum_scatter(
            ln1_gain_part.astype(jnp.bfloat16), "fsdp", scatter_dimension=0, tiled=True
        ).astype(jnp.float32),
        lax.psum_scatter(
            ln1_bias_part.astype(jnp.bfloat16), "fsdp", scatter_dimension=0, tiled=True
        ).astype(jnp.float32),
        lax.psum_scatter(
            w_qkv_part.astype(jnp.bfloat16), "fsdp", scatter_dimension=0, tiled=True
        ).astype(jnp.float32),
        lax.psum_scatter(
            q_bias_part.astype(jnp.bfloat16), "fsdp", scatter_dimension=0, tiled=True
        ).astype(jnp.float32),
        lax.psum_scatter(
            v_bias_part.astype(jnp.bfloat16), "fsdp", scatter_dimension=0, tiled=True
        ).astype(jnp.float32),
        lax.psum_scatter(
            w_out_part.astype(jnp.bfloat16), "fsdp", scatter_dimension=0, tiled=True
        ).astype(jnp.float32),
        lax.psum_scatter(
            out_bias_part.astype(jnp.bfloat16), "fsdp", scatter_dimension=0, tiled=True
        ).astype(jnp.float32),
        lax.psum_scatter(
            ln2_gain_part.astype(jnp.bfloat16), "fsdp", scatter_dimension=0, tiled=True
        ).astype(jnp.float32),
        lax.psum_scatter(
            ln2_bias_part.astype(jnp.bfloat16), "fsdp", scatter_dimension=0, tiled=True
        ).astype(jnp.float32),
        lax.psum_scatter(
            w_fc1_part.astype(jnp.bfloat16), "fsdp", scatter_dimension=0, tiled=True
        ).astype(jnp.float32),
        lax.psum_scatter(
            fc1_bias_part.astype(jnp.bfloat16), "fsdp", scatter_dimension=0, tiled=True
        ).astype(jnp.float32),
        lax.psum_scatter(
            w_fc2_part.astype(jnp.bfloat16), "fsdp", scatter_dimension=0, tiled=True
        ).astype(jnp.float32),
        lax.psum_scatter(
            fc2_bias_part.astype(jnp.bfloat16), "fsdp", scatter_dimension=0, tiled=True
        ).astype(jnp.float32),
    )
    summed = (
        lax.psum_scatter(
            partial_sums[0].astype(jnp.bfloat16), "seq", scatter_dimension=0, tiled=True
        ).astype(jnp.float32),
        lax.psum_scatter(
            partial_sums[1].astype(jnp.bfloat16), "seq", scatter_dimension=0, tiled=True
        ).astype(jnp.float32),
        lax.psum_scatter(
            partial_sums[2].astype(jnp.bfloat16), "seq", scatter_dimension=1, tiled=True
        ).astype(jnp.float32),
        lax.psum_scatter(
            partial_sums[3].astype(jnp.bfloat16), "seq", scatter_dimension=0, tiled=True
        ).astype(jnp.float32),
        lax.psum_scatter(
            partial_sums[4].astype(jnp.bfloat16), "seq", scatter_dimension=0, tiled=True
        ).astype(jnp.float32),
        lax.psum_scatter(
            partial_sums[5].astype(jnp.bfloat16), "seq", scatter_dimension=1, tiled=True
        ).astype(jnp.float32),
        lax.psum_scatter(
            partial_sums[6].astype(jnp.bfloat16), "seq", scatter_dimension=0, tiled=True
        ).astype(jnp.float32),
        lax.psum_scatter(
            partial_sums[7].astype(jnp.bfloat16), "seq", scatter_dimension=0, tiled=True
        ).astype(jnp.float32),
        lax.psum_scatter(
            partial_sums[8].astype(jnp.bfloat16), "seq", scatter_dimension=0, tiled=True
        ).astype(jnp.float32),
        lax.psum_scatter(
            partial_sums[9].astype(jnp.bfloat16), "seq", scatter_dimension=1, tiled=True
        ).astype(jnp.float32),
        lax.psum_scatter(
            partial_sums[10].astype(jnp.bfloat16), "seq", scatter_dimension=0, tiled=True
        ).astype(jnp.float32),
        lax.psum_scatter(
            partial_sums[11].astype(jnp.bfloat16), "seq", scatter_dimension=1, tiled=True
        ).astype(jnp.float32),
        lax.psum_scatter(
            partial_sums[12].astype(jnp.bfloat16), "seq", scatter_dimension=0, tiled=True
        ).astype(jnp.float32),
    )
    return (
        layer_output,
        tokens_grad,
        summed[0],
        summed[1],
        summed[2],
        summed[3],
        summed[4],
        summed[5],
        summed[6],
        summed[7],
        summed[8],
        summed[9],
        summed[10],
        summed[11],
        summed[12],
    )


def solution(mesh):
    return jax.shard_map(
        shards,
        mesh=mesh,
        in_specs=(
            P(("fsdp", "seq"), None),
            P(("fsdp", "seq")),
            P("fsdp"),
            P("fsdp"),
            P("fsdp", None),
            P("fsdp"),
            P("fsdp"),
            P("fsdp", None),
            P("fsdp"),
            P("fsdp"),
            P("fsdp"),
            P("fsdp", None),
            P("fsdp"),
            P("fsdp", None),
            P("fsdp"),
            P(("fsdp", "seq"), None),
        ),
        out_specs=(
            P(("fsdp", "seq"), None),
            P(("fsdp", "seq"), None),
            P(("fsdp", "seq")),
            P(("fsdp", "seq")),
            P("fsdp", "seq"),
            P(("fsdp", "seq")),
            P(("fsdp", "seq")),
            P("fsdp", "seq"),
            P(("fsdp", "seq")),
            P(("fsdp", "seq")),
            P(("fsdp", "seq")),
            P("fsdp", "seq"),
            P(("fsdp", "seq")),
            P("fsdp", "seq"),
            P(("fsdp", "seq")),
        ),
        check_vma=False,
    )
```

profile of v0, /device:TPU:0, one launch (start us, length us, event | category | flops | bytes accessed | tf_op | source)
XLA Modules:
  0.0 857.5 jit_solution(11295137797014356997)
XLA Ops:
  9.4 10.3 %all-gather.3 = bf16[8,1,128]{2,1,0:T(2,128)(2,1)S(1)} all-gather(bf16[1,1,128]{2,1,0:T(2,128)(2,1)} %bitcast.145), channel_id=1, replica_groups=mesh['fsdp'=8,'seq'=4] {'fsdp'}, dimensions={0}, use_global_device_ids=true | all-gather | bytes 2304 | tf_op jit(solution)/shard_map/all_gather | solution.py:87
  19.7 8.6 %all-gather.2 = bf16[8,1,128]{2,1,0:T(2,128)(2,1)S(1)} all-gather(bf16[1,1,128]{2,1,0:T(2,128)(2,1)} %bitcast.146), channel_id=1, replica_groups=mesh['fsdp'=8,'seq'=4] {'fsdp'}, dimensions={0}, use_global_device_ids=true | all-gather | bytes 2304 | tf_op jit(solution)/shard_map/all_gather | solution.py:86
  28.3 7.9 all-gather.1
  36.2 8.6 %all-gather = bf16[8,1,128]{2,1,0:T(2,128)(2,1)S(1)} all-gather(bf16[1,1,128]{2,1,0:T(2,128)(2,1)} %bitcast.148), channel_id=1, replica_groups=mesh['fsdp'=8,'seq'=4] {'fsdp'}, dimensions={0}, use_global_device_ids=true | all-gather | bytes 2304 | tf_op jit(solution)/shard_map/all_gather | solution.py:83
  47.1 11.1 %all-gather.15.cloned.1.call-done = bf16[1024,3072]{1,0:T(8,128)(2,1)} async-done(((bf16[128,3072]{1,0:T(8,128)(2,1)}), bf16[1024,3072]{1,0:T(8,128)(2,1)}) %all-gather.15.cloned.1.call-update) | async-done | bytes 6291472 | tf_op jit(solution)/shard_map/all_gather | solution.py:85
  58.2 6.9 add_convert_fusion.1
  65.1 3.0 copy.73
  68.1 3.7 copy.74
  71.8 4.7 all-to-all-start
  77.1 75.7 %all-gather.4 = s32[4,1,384]{2,1,0:T(1,128)S(1)} all-gather(s32[1,1,384]{2,1,0:T(1,128)S(1)} %reshape.224), channel_id=1, replica_groups=mesh['fsdp'=8,'seq'=4] {'seq'}, dimensions={0}, use_global_device_ids=true | all-gather | bytes 7680 | tf_op jit(solution)/shard_map/all_gather | solution.py:91
  165.7 81.2 %while.26 = (s32[]{:T(128)}, bf16[2,768,4,64]{1,3,2,0:T(8,128)(2,1)}, f32[2,4,768]{2,1,0:T(4,128)S(1)}, s32[2]{0:T(128)S(1)}, bf16[2688,4,64]{0,2,1:T(8,128)(2,1...) while((s32[]{:T(128)}, ...), condition=%wide.region_5.6_spmd, body=%wide.region_2.5_spmd.sunk | while | flops 1582396416 | bytes 85851936 | solution.py:142
  170.6 12.1 %fusion.119 = (f32[4,768]{1,0:T(4,128)S(1)}, f32[4,768,1920]{2,1,0:T(8,128)}) fusion(pred[768,1920]{1,0:T(8,128)(4,1)S(1)} %broadcast_compare_fusion.4, bf16[2688,4,64]{0,2,1:T(8,128)(2,1)S(1)} %get-tuple-element.433, s32[]{:T(128)S(6)} %select_n.71, bf16[1536,4,64]{0,2,1:T(8,128)(2,1)} %get-tuple-element.432, s32[]{:T(128)S(6)} %select_n.72), kind=kOutput, calls=%fused_computation.3.clone.1 | convolution fusion | flops 772666368 | bytes 26456072 | tf_op jit(solution)/shard_map/while/body/eval_jaxpr/qhd,khd->hqk/dot_general | solution.py:120
  182.6 11.3 %fusion.120 = f32[4,768]{1,0:T(4,128)S(1)} fusion(f32[4,768,1920]{2,1,0:T(8,128)} %get-tuple-element.383, f32[4,768]{1,0:T(4,128)S(1)} %get-tuple-element.384, pred[768,1920]{1,0:T(8,128)(4,1)S(1)} %broadcast_compare_fusion.4), kind=kLoop, calls=%fused_computation.4.clone.1 | loop fusion | flops 23589888 | bytes 25092096 | tf_op jit(solution)/shard_map/while/body/eval_jaxpr/reduce_sum | solution.py:135
  193.9 11.6 %fusion.121 = bf16[2,768,4,64]{1,3,2,0:T(8,128)(2,1)S(1)} fusion(bf16[2,768,4,64]{1,3,2,0:T(8,128)(2,1)S(1)} %copy-done.17, s32[]{:T(128)S(6)} %copy.99, f32[4,768,1920]{2,1,0:T(8,128)} %get-tuple-element.383, f32[4,768]{1,0:T(4,128)S(1)} %fusion.120, f32[4,768]{1,0:T(4,128)S(1)} %get-tuple-element.384, ...), kind=kOutput, calls=%fused_computation.9.clone.1 | convolution fusion | flops 784662528 | bytes 26468360 | tf_op jit(solution)/shard_map/while/body/eval_jaxpr/hqk,khd->qhd/dot_general | solution.py:137
  211.3 11.9 %fusion.119 = (f32[4,768]{1,0:T(4,128)S(1)}, f32[4,768,1920]{2,1,0:T(8,128)}) fusion(pred[768,1920]{1,0:T(8,128)(4,1)S(1)} %broadcast_compare_fusion.4, bf16[2688,4,64]{0,2,1:T(8,128)(2,1)S(1)} %get-tuple-element.433, s32[]{:T(128)S(6)} %select_n.71, bf16[1536,4,64]{0,2,1:T(8,128)(2,1)} %get-tuple-element.432, s32[]{:T(128)S(6)} %select_n.72), kind=kOutput, calls=%fused_computation.3.clone.1 | convolution fusion | flops 772666368 | bytes 26456072 | tf_op jit(solution)/shard_map/while/body/eval_jaxpr/qhd,khd->hqk/dot_general | solution.py:120
  223.2 11.1 %fusion.120 = f32[4,768]{1,0:T(4,128)S(1)} fusion(f32[4,768,1920]{2,1,0:T(8,128)} %get-tuple-element.383, f32[4,768]{1,0:T(4,128)S(1)} %get-tuple-element.384, pred[768,1920]{1,0:T(8,128)(4,1)S(1)} %broadcast_compare_fusion.4), kind=kLoop, calls=%fused_computation.4.clone.1 | loop fusion | flops 23589888 | bytes 25092096 | tf_op jit(solution)/shard_map/while/body/eval_jaxpr/reduce_sum | solution.py:135
  234.3 11.7 %fusion.121 = bf16[2,768,4,64]{1,3,2,0:T(8,128)(2,1)S(1)} fusion(bf16[2,768,4,64]{1,3,2,0:T(8,128)(2,1)S(1)} %copy-done.17, s32[]{:T(128)S(6)} %copy.99, f32[4,768,1920]{2,1,0:T(8,128)} %get-tuple-element.383, f32[4,768]{1,0:T(4,128)S(1)} %fusion.120, f32[4,768]{1,0:T(4,128)S(1)} %get-tuple-element.384, ...), kind=kOutput, calls=%fused_computation.9.clone.1 | convolution fusion | flops 784662528 | bytes 26468360 | tf_op jit(solution)/shard_map/while/body/eval_jaxpr/hqk,khd->qhd/dot_general | solution.py:137
  249.8 3.3 all_to_all.54
  255.2 4.4 all-to-all-start.1
  259.6 9.1 %all-gather.5 = bf16[8,1,128]{2,1,0:T(2,128)(2,1)S(1)} all-gather(bf16[1,1,128]{2,1,0:T(2,128)(2,1)S(1)} %bitcast.149), channel_id=1, replica_groups=mesh['fsdp'=8,'seq'=4] {'fsdp'}, dimensions={0}, use_global_device_ids=true | all-gather | bytes 2304 | tf_op jit(solution)/shard_map/all_gather | solution.py:89
  268.7 8.3 all-gather.8
  277.1 8.4 all-gather.7
  285.4 8.1 all-gather.6
  293.6 3.1 fusion.80
  298.2 20.9 %multiply_convert_fusion.1 = (bf16[384,4096]{1,0:T(8,128)(2,1)}, f32[384,4096]{1,0:T(8,128)}, f32[384,4096]{1,0:T(8,128)}) fusion(f32[4096]{0:T(1024)S(1)} %bitcast.133, bf16[1024,4096]{1,0:T(8,128)(2,1)} %all-gather.19.cloned.1.call-done, f32[384,1024]{1,0:T(8,128)} %copy-done.11, f32[1024]{0:T(1024)S(1)} %bitcast.142, f32[1024]{0:T(1024)S(1)} %bitcast.136, ...), kind=kOutput, calls=%fused_computation.56 | convolution fusion | flops 3327000576 | bytes 25717760 | tf_op jit(solution)/shard_map/dot_general | solution.py:160
  319.1 11.8 %fusion.81 = (bf16[4096]{0:T(1024)(128)(2,1)}, bf16[384,4096]{1,0:T(8,128)(2,1)S(1)}) fusion(f32[384,4096]{1,0:T(8,128)} %get-tuple-element.239, f32[384,4096]{1,0:T(8,128)} %get-tuple-element.250, bf16[4096,1024]{1,0:T(8,128)(2,1)} %all-gather.21.cloned.1.call-done, bf16[384,1024]{1,0:T(8,128)(2,1)} %param.35, f32[384]{0:T(512)S(1)} %compare_convert_fusion), kind=kOutput, calls=%fused_computation.137 | convolution fusion | flops 3245993984 | bytes 24913408 | tf_op jit(solution)/shard_map/dot_general | solution.py:27
  330.9 4.3 multiply_reduce_fusion.1
  338.8 3.7 convolution_convert_fusion.3
  342.7 10.4 %convolution_convert_fusion.1 = bf16[1024,4096]{1,0:T(8,128)(2,1)} fusion(bf16[384,4096]{1,0:T(8,128)(2,1)} %copy-done.50, f32[384,1024]{1,0:T(8,128)} %copy-done.11, f32[1024]{0:T(1024)S(1)} %bitcast.143, f32[1024]{0:T(1024)S(1)} %bitcast.139, f32[384]{0:T(512)S(1)} %fusion.64, f32[384]{0:T(512)S(1)} %broadcast_multiply_fusion), kind=kOutput, calls=%fused_computation.53 | convolution fusion | flops 3227385856 | bytes 13118464 | tf_op jit(solution)/shard_map/dot_general | solution.py:21
  353.1 3.0 convolution_convert_fusion.4
  357.1 5.0 all-to-all-start.2
  362.1 10.0 %convolution_convert_fusion = bf16[4096,1024]{1,0:T(8,128)(2,1)} fusion(bf16[384,4096]{1,0:T(8,128)(2,1)} %get-tuple-element.238, bf16[384,1024]{1,0:T(8,128)(2,1)} %param.35, f32[384]{0:T(512)S(1)} %compare_convert_fusion), kind=kOutput, calls=%fused_computation.52 | convolution fusion | flops 3226599424 | bytes 12322304 | tf_op jit(solution)/shard_map/dot_general | solution.py:21
  372.1 10.6 %all-to-all-done.2 = bf16[384,4,256]{2,0,1:T(8,128)(2,1)} async-done(((bf16[384,4,256]{2,0,1:T(8,128)(2,1)}), bf16[384,4,256]{2,0,1:T(8,128)(2,1)}, u32[]{:S(2)}, u32[]{:S(2)}) %all-to-all-start.2) | async-done | bytes 786464 | tf_op jit(solution)/shard_map/all_to_all | solution.py:188
  390.8 214.2 %while.27 = (s32[]{:T(128)}, f32[2688,4,64]{0,2,1:T(8,128)}, f32[2688,4,64]{0,2,1:T(8,128)}, bf16[2,768,4,64]{1,3,2,0:T(8,128)(2,1)}, s32[2]{0:T(128)S(1)}, /*in...) while((s32[]{:T(128)}, f32[2688,4,64]{0,2,1:T(8,128)}, ...), condition=%wide.region_12.13_spmd, body=%wide.region_10.12_spmd.sunk | while | flops 3866489856 | bytes 287363040 | solution.py:224
  394.9 13.9 %fusion.130 = f32[4,768,1920]{2,1,0:T(8,128)} fusion(bf16[2688,4,64]{0,2,1:T(8,128)(2,1)S(1)} %get-tuple-element.478, s32[]{:T(128)S(6)} %select_n.76, bf16[1536,4,64]{0,2,1:T(8,128)(2,1)} %get-tuple-element.475, s32[]{:T(128)S(6)} %select_n.77), kind=kOutput, calls=%fused_computation.37.clone.1 | convolution fusion | flops 754974720 | bytes 24969224 | tf_op jit(solution)/shard_map/while/body/eval_jaxpr/qhd,khd->hqk/dot_general | solution.py:120
  409.9 22.2 %multiply_reduce_fusion.5 = (f32[4,768]{1,0:T(4,128)S(1)}, f32[4,768,1920]{2,1,0:T(8,128)}) fusion(f32[4,768,1920]{2,1,0:T(8,128)} %fusion.130, f32[4,768]{1,0:T(4,128)S(1)} %dynamic-slice_bitcast_fusion.2, pred[768,1920]{1,0:T(8,128)(4,1)S(1)} %broadcast_compare_fusion.5, bf16[2688,4,64]{0,2,1:T(8,128)(2,1)S(1)} %get-tuple-element.481, ...), kind=kOutput, calls=%fused_computation.20.clone.1 | convolution fusion | flops 784462848 | bytes 50061320 | tf_op jit(solution)/shard_map/while/body/eval_jaxpr/qhd,khd->hqk/dot_general | solution.py:202
  432.1 17.7 %multiply_convert_fusion.4 = bf16[4,768,1920]{2,1,0:T(8,128)(2,1)S(1)} fusion(f32[4,768,1920]{2,1,0:T(8,128)} %get-tuple-element.397, f32[4,768,1920]{2,1,0:T(8,128)} %fusion.130, f32[4,768]{1,0:T(4,128)S(1)} %get-tuple-element.398, f32[4,768]{1,0:T(4,128)S(1)} %dynamic-slice_bitcast_fusion.2, pred[768,1920]{1,0:T(8,128)(4,1)S(1)} %broadcast_compare_fusion.5), kind=kLoop, calls=%fused_computation.19.clone.1 | loop fusion | flops 35389440 | bytes 60481536 | tf_op jit(solution)/shard_map/while/body/eval_jaxpr/convert_element_type | solution.py:206
  449.8 4.3 copy-done
  456.1 10.0 %dynamic_update_slice.29 = f32[2688,4,64]{0,2,1:T(8,128)} dynamic-update-slice(f32[2688,4,64]{0,2,1:T(8,128)} %get-tuple-element.455, f32[1920,4,64]{0,2,1:T(8,128)S(1)} %fusion.131, s32[]{:T(128)S(6)} %select_n.76, s32[]{:T(128)} %constant.72.clone.1..sunk.1, s32[]{:T(128)} %constant.72.clone.1..sunk.1) | dynamic-update-slice | bytes 3932164 | tf_op jit(solution)/shard_map/while/body/eval_jaxpr/dynamic_update_slice | solution.py:45
  466.1 16.1 %fusion.132 = f32[1920,4,64]{0,2,1:T(8,128)S(1)} fusion(f32[4,768,1920]{2,1,0:T(8,128)} %fusion.130, f32[4,768]{1,0:T(4,128)S(1)} %dynamic-slice_bitcast_fusion.2, pred[768,1920]{1,0:T(8,128)(4,1)S(1)} %broadcast_compare_fusion.5, f32[2688,4,64]{0,2,1:T(8,128)} %get-tuple-element.456, s32[]{:T(128)S(6)} %select_n.76, ...), kind=kOutput, calls=%fused_computation.30.clone.1 | convolution fusion | flops 779059200 | bytes 29405192 | tf_op jit(solution)/shard_map/while/body/eval_jaxpr/hqk,qhd->khd/dot_general | solution.py:199
  482.2 10.2 %dynamic_update_slice.30 = f32[2688,4,64]{0,2,1:T(8,128)} dynamic-update-slice(f32[2688,4,64]{0,2,1:T(8,128)} %get-tuple-element.456, f32[1920,4,64]{0,2,1:T(8,128)S(1)} %fusion.132, s32[]{:T(128)S(6)} %select_n.76, s32[]{:T(128)} %constant.72.clone.1..sunk.1, s32[]{:T(128)} %constant.72.clone.1..sunk.1) | dynamic-update-slice | bytes 3932164 | tf_op jit(solution)/shard_map/while/body/eval_jaxpr/dynamic_update_slice | solution.py:45
  492.4 9.2 %fusion.133 = bf16[2,768,4,64]{1,3,2,0:T(8,128)(2,1)} fusion(bf16[2,768,4,64]{1,3,2,0:T(8,128)(2,1)} %get-tuple-element.457, s32[]{:T(128)S(6)} %copy.109, bf16[4,768,1920]{2,1,0:T(8,128)(2,1)} %copy-done, bf16[2688,4,64]{0,2,1:T(8,128)(2,1)S(1)} %copy-done.2, s32[]{:T(128)S(6)} %select_n.76), kind=kOutput, calls=%fused_computation.33.clone.1 | convolution fusion | flops 755171328 | bytes 13565960 | tf_op jit(solution)/shard_map/while/body/eval_jaxpr/hqk,khd->qhd/dot_general | solution.py:208
  505.5 12.3 %fusion.130 = f32[4,768,1920]{2,1,0:T(8,128)} fusion(bf16[2688,4,64]{0,2,1:T(8,128)(2,1)S(1)} %get-tuple-element.478, s32[]{:T(128)S(6)} %select_n.76, bf16[1536,4,64]{0,2,1:T(8,128)(2,1)} %get-tuple-element.475, s32[]{:T(128)S(6)} %select_n.77), kind=kOutput, calls=%fused_computation.37.clone.1 | convolution fusion | flops 754974720 | bytes 24969224 | tf_op jit(solution)/shard_map/while/body/eval_jaxpr/qhd,khd->hqk/dot_general | solution.py:120
  519.0 22.2 %multiply_reduce_fusion.5 = (f32[4,768]{1,0:T(4,128)S(1)}, f32[4,768,1920]{2,1,0:T(8,128)}) fusion(f32[4,768,1920]{2,1,0:T(8,128)} %fusion.130, f32[4,768]{1,0:T(4,128)S(1)} %dynamic-slice_bitcast_fusion.2, pred[768,1920]{1,0:T(8,128)(4,1)S(1)} %broadcast_compare_fusion.5, bf16[2688,4,64]{0,2,1:T(8,128)(2,1)S(1)} %get-tuple-element.481, ...), kind=kOutput, calls=%fused_computation.20.clone.1 | convolution fusion | flops 784462848 | bytes 50061320 | tf_op jit(solution)/shard_map/while/body/eval_jaxpr/qhd,khd->hqk/dot_general | solution.py:202
  541.2 17.0 %multiply_convert_fusion.4 = bf16[4,768,1920]{2,1,0:T(8,128)(2,1)S(1)} fusion(f32[4,768,1920]{2,1,0:T(8,128)} %get-tuple-element.397, f32[4,768,1920]{2,1,0:T(8,128)} %fusion.130, f32[4,768]{1,0:T(4,128)S(1)} %get-tuple-element.398, f32[4,768]{1,0:T(4,128)S(1)} %dynamic-slice_bitcast_fusion.2, pred[768,1920]{1,0:T(8,128)(4,1)S(1)} %broadcast_compare_fusion.5), kind=kLoop, calls=%fused_computation.19.clone.1 | loop fusion | flops 35389440 | bytes 60481536 | tf_op jit(solution)/shard_map/while/body/eval_jaxpr/convert_element_type | solution.py:206
  558.3 4.3 copy-done
  564.6 9.4 %dynamic_update_slice.29 = f32[2688,4,64]{0,2,1:T(8,128)} dynamic-update-slice(f32[2688,4,64]{0,2,1:T(8,128)} %get-tuple-element.455, f32[1920,4,64]{0,2,1:T(8,128)S(1)} %fusion.131, s32[]{:T(128)S(6)} %select_n.76, s32[]{:T(128)} %constant.72.clone.1..sunk.1, s32[]{:T(128)} %constant.72.clone.1..sunk.1) | dynamic-update-slice | bytes 3932164 | tf_op jit(solution)/shard_map/while/body/eval_jaxpr/dynamic_update_slice | solution.py:45
  574.0 12.3 %fusion.132 = f32[1920,4,64]{0,2,1:T(8,128)S(1)} fusion(f32[4,768,1920]{2,1,0:T(8,128)} %fusion.130, f32[4,768]{1,0:T(4,128)S(1)} %dynamic-slice_bitcast_fusion.2, pred[768,1920]{1,0:T(8,128)(4,1)S(1)} %broadcast_compare_fusion.5, f32[2688,4,64]{0,2,1:T(8,128)} %get-tuple-element.456, s32[]{:T(128)S(6)} %select_n.76, ...), kind=kOutput, calls=%fused_computation.30.clone.1 | convolution fusion | flops 779059200 | bytes 29405192 | tf_op jit(solution)/shard_map/while/body/eval_jaxpr/hqk,qhd->khd/dot_general | solution.py:199
  586.4 9.5 %dynamic_update_slice.30 = f32[2688,4,64]{0,2,1:T(8,128)} dynamic-update-slice(f32[2688,4,64]{0,2,1:T(8,128)} %get-tuple-element.456, f32[1920,4,64]{0,2,1:T(8,128)S(1)} %fusion.132, s32[]{:T(128)S(6)} %select_n.76, s32[]{:T(128)} %constant.72.clone.1..sunk.1, s32[]{:T(128)} %constant.72.clone.1..sunk.1) | dynamic-update-slice | bytes 3932164 | tf_op jit(solution)/shard_map/while/body/eval_jaxpr/dynamic_update_slice | solution.py:45
  595.9 8.9 %fusion.133 = bf16[2,768,4,64]{1,3,2,0:T(8,128)(2,1)} fusion(bf16[2,768,4,64]{1,3,2,0:T(8,128)(2,1)} %get-tuple-element.457, s32[]{:T(128)S(6)} %copy.109, bf16[4,768,1920]{2,1,0:T(8,128)(2,1)} %copy-done, bf16[2688,4,64]{0,2,1:T(8,128)(2,1)S(1)} %copy-done.2, s32[]{:T(128)S(6)} %select_n.76), kind=kOutput, calls=%fused_computation.33.clone.1 | convolution fusion | flops 755171328 | bytes 13565960 | tf_op jit(solution)/shard_map/while/body/eval_jaxpr/hqk,khd->qhd/dot_general | solution.py:208
  613.3 3.6 copy.85
  616.9 3.7 all-to-all-start.3
  621.4 74.2 %all-to-all-done.3 = bf16[1536,3,256]{2,1,0:T(4,128)(2,1)S(1)} async-done(((bf16[1536,3,256]{2,1,0:T(4,128)(2,1)}), bf16[1536,3,256]{2,1,0:T(4,128)(2,1)S(1)}, u32[]{:S(2)}, u32[]{:S(2)}) %all-to-all-start.3) | async-done | bytes 2359328 | tf_op jit(solution)/shard_map/all_to_all | solution.py:237
  697.4 3.1 copy.87
  700.5 5.9 convolution_convert_fusion.2
  707.9 8.6 %all-gather.9 = bf16[8,1,128]{2,1,0:T(2,128)(2,1)S(1)} all-gather(bf16[1,1,128]{2,1,0:T(2,128)(2,1)S(1)} %bitcast.152), channel_id=1, replica_groups=mesh['fsdp'=8,'seq'=4] {'fsdp'}, dimensions={0}, use_global_device_ids=true | all-gather | bytes 2304 | tf_op jit(solution)/shard_map/all_gather | solution.py:155
  720.3 8.8 %multiply_convert_fusion.2 = bf16[384,1024]{1,0:T(8,128)(2,1)} fusion(f32[384,1024]{1,0:T(8,128)S(1)} %copy-done.13, bf16[384,4096]{1,0:T(8,128)(2,1)} %get-tuple-element.238, bf16[4096,1024]{1,0:T(8,128)(2,1)} %all-gather.21.cloned.1.call-done, f32[1024]{0:T(1024)S(1)} %bitcast.144, f32[384]{0:T(512)S(1)} %copy-done.26), kind=kOutput, calls=%fused_computation.99 | convolution fusion | flops 3222798336 | bytes 13899264 | tf_op jit(solution)/shard_map/dot_general | solution.py:164
  730.6 7.4 fusion.74
  738.2 28.6 %reduce-scatter.9.cloned.1.call-done = bf16[128,3072]{1,0:T(8,128)(2,1)} async-done(((bf16[1024,3072]{1,0:T(8,128)(2,1)}), bf16[128,3072]{1,0:T(8,128)(2,1)}) %reduce-scatter.9.cloned.1.call-update) | async-done | bytes 786448 | tf_op jit(solution)/shard_map/reduce_scatter | solution.py:256
  770.7 23.8 %all-reduce.21 = (bf16[1024]{0:T(1024)(128)(2,1)S(1)}, bf16[1024]{0:T(1024)(128)(2,1)S(1)}, bf16[1024]{0:T(1024)(128)(2,1)S(1)}, bf16[1024]{0:T(1024)(128)(2,1)S...) all-reduce(bf16[1024]{0:T(1024)(128)(2,1)S(1)} %get-tuple-element.1, ...), channel_id=2, replica_groups=mesh['fsdp'=8,'seq'=4] {'fsdp'}, use_global_device_ids=true, to_apply=%region_16.17.clone | all-reduce | flops 12288 | bytes 49152
  795.2 12.5 %all-reduce.22 = (bf16[128]{0:T(256)(128)(2,1)S(1)}, bf16[128]{0:T(256)(128)(2,1)S(1)}, bf16[128]{0:T(256)(128)(2,1)S(1)}, bf16[128]{0:T(256)(128)(2,1)S(1)}, bf...) all-reduce(bf16[128]{0:T(256)(128)(2,1)S(1)} %dynamic-slice.1, ...), channel_id=3, replica_groups=mesh['fsdp'=8,'seq'=4] {'seq'}, use_global_device_ids=true, to_apply=%region_17.18.clone | all-reduce | flops 1536 | bytes 6144
  810.6 3.3 add_add_fusion.2
  815.7 8.6 %reduce-scatter.23.cloned.1.call-done = bf16[512,256]{1,0:T(8,128)(2,1)} async-done(((bf16[512,1024]{1,0:T(8,128)(2,1)}), bf16[512,256]{1,0:T(8,128)(2,1)}) %reduce-scatter.23.cloned.1.call-update) | async-done | bytes 262160 | tf_op jit(solution)/shard_map/reduce_scatter | solution.py:324
  826.1 22.4 %reduce-scatter.11.cloned.1.call-done = bf16[128,768]{1,0:T(8,128)(2,1)} async-done(((bf16[128,3072]{1,0:T(8,128)(2,1)}), bf16[128,768]{1,0:T(8,128)(2,1)}) %reduce-scatter.11.cloned.1.call-update) | async-done | bytes 196624 | tf_op jit(solution)/shard_map/reduce_scatter | solution.py:297
  (251 shorter events, 77.4 us)
Async XLA Ops:
  7.2 39.0 %copy-start.7 = (bf16[384,1024]{1,0:T(8,128)(2,1)S(1)}, bf16[384,1024]{1,0:T(8,128)(2,1)}, u32[]{:S(2)}) copy-start(bf16[384,1024]{1,0:T(8,128)(2,1)} %param.20) | copy-start | bytes 2359300
  7.2 51.0 %all-gather.15.cloned.1.call-start = ((), (), s32[]{:S(2)}) async-start(), calls=%async_computation.12 | async-start | bytes 7077888 | tf_op jit(solution)/shard_map/all_gather | solution.py:85
  7.9 285.7 %all-gather.17.cloned.1.call-start = ((), (), s32[]{:S(2)}) async-start(), calls=%async_computation.13 | async-start | bytes 2359296 | tf_op jit(solution)/shard_map/all_gather | solution.py:88
  8.7 289.5 %all-gather.19.cloned.1.call-start = ((), (), s32[]{:S(2)}) async-start(), calls=%async_computation.14 | async-start | bytes 9437184 | tf_op jit(solution)/shard_map/all_gather | solution.py:152
  36.2 22.0 %copy-start.38 = (f32[8,1,128]{2,1,0:T(1,128)}, f32[8,1,128]{2,1,0:T(1,128)S(1)}, u32[]{:S(2)}) copy-start(f32[8,1,128]{2,1,0:T(1,128)S(1)} %convert_element_type.226) | copy-start | bytes 12292
  44.8 13.4 %copy-start.21 = (f32[8,1,128]{2,1,0:T(1,128)}, f32[8,1,128]{2,1,0:T(1,128)S(1)}, u32[]{:S(2)}) copy-start(f32[8,1,128]{2,1,0:T(1,128)S(1)} %convert_element_type.225) | copy-start | bytes 12292
  46.2 12.0 %copy-start.23 = (f32[384]{0:T(512)}, f32[384]{0:T(512)S(1)}, u32[]{:S(2)}) copy-start(f32[384]{0:T(512)S(1)} %broadcast_multiply_fusion.1) | copy-start | bytes 4612
  47.1 11.1 %copy-start.31 = (f32[384]{0:T(512)}, f32[384]{0:T(512)S(1)}, u32[]{:S(2)}) copy-start(f32[384]{0:T(512)S(1)} %fusion.63) | copy-start | bytes 4612
  71.8 5.3 copy-start.36
  71.8 81.2 %all-to-all-start = ((bf16[384,3,1024]{0,1,2:T(4,128)(2,1)}), bf16[384,3,1024]{0,1,2:T(4,128)(2,1)S(1)}, u32[]{:S(2)}, u32[]{:S(2)}) async-start(bf16[384,3,1024]{0,1,2:T(4,128)(2,1)} %copy.74), calls=%async_computation | async-start | bytes 6291456 | tf_op jit(solution)/shard_map/all_to_all | solution.py:105
  76.5 242.6 %all-gather.21.cloned.1.call-start = ((), (), s32[]{:S(2)}) async-start(), calls=%async_computation.15 | async-start | bytes 9437184 | tf_op jit(solution)/shard_map/all_gather | solution.py:154
  182.6 11.3 %copy-start.17 = (bf16[2,768,4,64]{1,3,2,0:T(8,128)(2,1)S(1)}, bf16[2,768,4,64]{1,3,2,0:T(8,128)(2,1)}, u32[]{:S(2)}) copy-start(bf16[2,768,4,64]{1,3,2,0:T(8,128)(2,1)} %get-tuple-element.413) | copy-start | bytes 2359300 | tf_op jit(solution)/shard_map/while
  223.2 11.1 %copy-start.17 = (bf16[2,768,4,64]{1,3,2,0:T(8,128)(2,1)S(1)}, bf16[2,768,4,64]{1,3,2,0:T(8,128)(2,1)}, u32[]{:S(2)}) copy-start(bf16[2,768,4,64]{1,3,2,0:T(8,128)(2,1)} %get-tuple-element.413) | copy-start | bytes 2359300 | tf_op jit(solution)/shard_map/while
  246.9 12.8 %copy-start.43 = (bf16[128]{0:T(256)(128)(2,1)S(1)}, bf16[128]{0:T(256)(128)(2,1)}, u32[]{:S(2)}) copy-start(bf16[128]{0:T(256)(128)(2,1)} %param.28) | copy-start | bytes 772
  246.9 21.8 %copy-start.42 = (bf16[512]{0:T(512)(128)(2,1)S(1)}, bf16[512]{0:T(512)(128)(2,1)}, u32[]{:S(2)}) copy-start(bf16[512]{0:T(512)(128)(2,1)} %param.32) | copy-start | bytes 3076
  246.9 30.2 %copy-start.44 = (bf16[128]{0:T(256)(128)(2,1)S(1)}, bf16[128]{0:T(256)(128)(2,1)}, u32[]{:S(2)}) copy-start(bf16[128]{0:T(256)(128)(2,1)} %param.30) | copy-start | bytes 772
  246.9 38.6 %copy-start.45 = (bf16[128]{0:T(256)(128)(2,1)S(1)}, bf16[128]{0:T(256)(128)(2,1)}, u32[]{:S(2)}) copy-start(bf16[128]{0:T(256)(128)(2,1)} %param.29) | copy-start | bytes 772
  246.9 46.7 %copy-start.37 = (s32[384]{0:T(512)S(1)}, s32[384]{0:T(512)}, u32[]{:S(2)}) copy-start(s32[384]{0:T(512)} %param.21) | copy-start | bytes 4612
  255.2 38.4 %all-to-all-start.1 = ((bf16[4,384,256]{1,2,0:T(8,128)(2,1)}), bf16[4,384,256]{1,2,0:T(8,128)(2,1)}, u32[]{:S(2)}, u32[]{:S(2)}) async-start(bf16[4,384,256]{1,2,0:T(8,128)(2,1)} %copy.81), calls=%async_computation.1 | async-start | bytes 1572864 | tf_op jit(solution)/shard_map/all_to_all | solution.py:144
  259.6 361.0 %reduce-scatter.13.cloned.1.call-start = ((), (), s32[]{:S(2)}) async-start(), calls=%async_computation.18 | async-start | bytes 2359296 | tf_op jit(solution)/shard_map/reduce_scatter | solution.py:265
  293.6 68.5 %copy-start.25 = (f32[384]{0:T(512)}, f32[384]{0:T(512)S(1)}, u32[]{:S(2)}) copy-start(f32[384]{0:T(512)S(1)} %compare_convert_fusion) | copy-start | bytes 4612
  319.1 11.8 %copy-start.12 = (f32[384,1024]{1,0:T(8,128)S(1)}, f32[384,1024]{1,0:T(8,128)}, u32[]{:S(2)}) copy-start(f32[384,1024]{1,0:T(8,128)} %copy-done.11) | copy-start | bytes 4718596
  319.1 11.8 %copy-start.47 = (bf16[1024,4096]{1,0:T(8,128)(2,1)S(1)}, bf16[1024,4096]{1,0:T(8,128)(2,1)}, u32[]{:S(2)}) copy-start(bf16[1024,4096]{1,0:T(8,128)(2,1)} %all-gather.19.cloned.1.call-done) | copy-start | bytes 25165828
  330.9 4.3 copy-start.50
  335.8 6.8 copy-start.27
  342.6 364.0 %reduce-scatter.17.cloned.1.call-start = ((), (), s32[]{:S(2)}) async-start(), calls=%async_computation.20 | async-start | bytes 9437184 | tf_op jit(solution)/shard_map/reduce_scatter | solution.py:277
  357.1 25.7 %all-to-all-start.2 = ((bf16[384,4,256]{2,0,1:T(8,128)(2,1)}), bf16[384,4,256]{2,0,1:T(8,128)(2,1)}, u32[]{:S(2)}, u32[]{:S(2)}) async-start(bf16[384,4,256]{2,0,1:T(8,128)(2,1)} %bitcast.123), calls=%async_computation.2 | async-start | bytes 1572864 | tf_op jit(solution)/shard_map/all_to_all | solution.py:188
  362.0 345.1 %reduce-scatter.21.cloned.1.call-start = ((), (), s32[]{:S(2)}) async-start(), calls=%async_computation.22 | async-start | bytes 9437184 | tf_op jit(solution)/shard_map/reduce_scatter | solution.py:283
  390.9 17.9 %copy-start.1 = (bf16[2688,4,64]{0,2,1:T(8,128)(2,1)}, bf16[2688,4,64]{0,2,1:T(8,128)(2,1)S(1)}, u32[]{:S(2)}) copy-start(bf16[2688,4,64]{0,2,1:T(8,128)(2,1)S(1)} %get-tuple-element.478) | copy-start | bytes 4128772 | tf_op jit(solution)/shard_map/while
  390.9 19.0 %copy-start.4 = (bf16[2688,4,64]{0,2,1:T(8,128)(2,1)}, bf16[2688,4,64]{0,2,1:T(8,128)(2,1)S(1)}, u32[]{:S(2)}) copy-start(bf16[2688,4,64]{0,2,1:T(8,128)(2,1)S(1)} %get-tuple-element.481) | copy-start | bytes 4128772 | tf_op jit(solution)/shard_map/while
  432.1 22.0 %copy-start.3 = (f32[2688,4,64]{0,2,1:T(8,128)S(1)}, f32[2688,4,64]{0,2,1:T(8,128)}, u32[]{:S(2)}) copy-start(f32[2688,4,64]{0,2,1:T(8,128)} %get-tuple-element.455) | copy-start | bytes 8257540 | tf_op jit(solution)/shard_map/while
  432.1 22.0 %copy-start.6 = (bf16[1536,4,64]{0,2,1:T(8,128)(2,1)S(1)}, bf16[1536,4,64]{0,2,1:T(8,128)(2,1)}, u32[]{:S(2)}) copy-start(bf16[1536,4,64]{0,2,1:T(8,128)(2,1)} %get-tuple-element.475) | copy-start | bytes 2359300 | tf_op jit(solution)/shard_map/while
  449.8 4.3 copy-start
  482.2 10.2 %copy-start.2 = (bf16[2688,4,64]{0,2,1:T(8,128)(2,1)S(1)}, bf16[2688,4,64]{0,2,1:T(8,128)(2,1)}, u32[]{:S(2)}) copy-start(bf16[2688,4,64]{0,2,1:T(8,128)(2,1)} %copy-done.1) | copy-start | bytes 4128772 | tf_op jit(solution)/shard_map/while
  492.4 9.2 %copy-start.5 = (bf16[2688,4,64]{0,2,1:T(8,128)(2,1)S(1)}, bf16[2688,4,64]{0,2,1:T(8,128)(2,1)}, u32[]{:S(2)}) copy-start(bf16[2688,4,64]{0,2,1:T(8,128)(2,1)} %copy-done.4) | copy-start | bytes 4128772 | tf_op jit(solution)/shard_map/while
  501.6 16.3 %copy-start.1 = (bf16[2688,4,64]{0,2,1:T(8,128)(2,1)}, bf16[2688,4,64]{0,2,1:T(8,128)(2,1)S(1)}, u32[]{:S(2)}) copy-start(bf16[2688,4,64]{0,2,1:T(8,128)(2,1)S(1)} %get-tuple-element.478) | copy-start | bytes 4128772 | tf_op jit(solution)/shard_map/while
  501.6 17.3 %copy-start.4 = (bf16[2688,4,64]{0,2,1:T(8,128)(2,1)}, bf16[2688,4,64]{0,2,1:T(8,128)(2,1)S(1)}, u32[]{:S(2)}) copy-start(bf16[2688,4,64]{0,2,1:T(8,128)(2,1)S(1)} %get-tuple-element.481) | copy-start | bytes 4128772 | tf_op jit(solution)/shard_map/while
  541.2 21.3 %copy-start.3 = (f32[2688,4,64]{0,2,1:T(8,128)S(1)}, f32[2688,4,64]{0,2,1:T(8,128)}, u32[]{:S(2)}) copy-start(f32[2688,4,64]{0,2,1:T(8,128)} %get-tuple-element.455) | copy-start | bytes 8257540 | tf_op jit(solution)/shard_map/while
  541.2 21.3 %copy-start.6 = (bf16[1536,4,64]{0,2,1:T(8,128)(2,1)S(1)}, bf16[1536,4,64]{0,2,1:T(8,128)(2,1)}, u32[]{:S(2)}) copy-start(bf16[1536,4,64]{0,2,1:T(8,128)(2,1)} %get-tuple-element.475) | copy-start | bytes 2359300 | tf_op jit(solution)/shard_map/while
  558.2 4.3 copy-start
  586.3 9.5 %copy-start.2 = (bf16[2688,4,64]{0,2,1:T(8,128)(2,1)S(1)}, bf16[2688,4,64]{0,2,1:T(8,128)(2,1)}, u32[]{:S(2)}) copy-start(bf16[2688,4,64]{0,2,1:T(8,128)(2,1)} %copy-done.1) | copy-start | bytes 4128772 | tf_op jit(solution)/shard_map/while
  595.9 8.9 %copy-start.5 = (bf16[2688,4,64]{0,2,1:T(8,128)(2,1)S(1)}, bf16[2688,4,64]{0,2,1:T(8,128)(2,1)}, u32[]{:S(2)}) copy-start(bf16[2688,4,64]{0,2,1:T(8,128)(2,1)} %copy-done.4) | copy-start | bytes 4128772 | tf_op jit(solution)/shard_map/while
  605.0 4.5 copy-start.19
  616.9 78.7 %all-to-all-start.3 = ((bf16[1536,3,256]{2,1,0:T(4,128)(2,1)}), bf16[1536,3,256]{2,1,0:T(4,128)(2,1)S(1)}, u32[]{:S(2)}, u32[]{:S(2)}) async-start(bf16[1536,3,256]{2,1,0:T(4,128)(2,1)} %copy.85), calls=%async_computation.3 | async-start | bytes 6291456 | tf_op jit(solution)/shard_map/all_to_all | solution.py:237
  620.6 108.5 %reduce-scatter.15.cloned.1.call-start = ((), (), s32[]{:S(2)}) async-start(), calls=%async_computation.19 | async-start | bytes 327680 | tf_op jit(solution)/shard_map/reduce_scatter | solution.py:306
  621.3 145.4 %reduce-scatter.9.cloned.1.call-start = ((), (), s32[]{:S(2)}) async-start(), calls=%async_computation.16 | async-start | bytes 7077888 | tf_op jit(solution)/shard_map/reduce_scatter | solution.py:256
  697.4 3.1 copy-start.39
  700.4 6.0 copy-start.14
  706.4 10.1 %copy-start.49 = (u32[32]{0:T(128)S(1)}, u32[32]{0:T(128)}, u32[]{:S(2)}) copy-start(u32[32]{0:T(128)} %constant.148) | copy-start | bytes 388
  706.5 10.7 %copy-start.48 = (u32[32]{0:T(128)S(1)}, u32[32]{0:T(128)}, u32[]{:S(2)}) copy-start(u32[32]{0:T(128)} %constant.152) | copy-start | bytes 388
  706.5 13.8 %copy-start.13 = (f32[384,1024]{1,0:T(8,128)S(1)}, f32[384,1024]{1,0:T(8,128)}, u32[]{:S(2)}) copy-start(f32[384,1024]{1,0:T(8,128)} %copy-done.11) | copy-start | bytes 4718596
  706.5 13.8 %copy-start.26 = (f32[384]{0:T(512)S(1)}, f32[384]{0:T(512)}, u32[]{:S(2)}) copy-start(f32[384]{0:T(512)} %copy-done.25) | copy-start | bytes 4612
  706.5 107.4 %reduce-scatter.19.cloned.1.call-start = ((), (), s32[]{:S(2)}) async-start(), calls=%async_computation.21 | async-start | bytes 1310720 | tf_op jit(solution)/shard_map/reduce_scatter | solution.py:318
  707.1 117.3 %reduce-scatter.23.cloned.1.call-start = ((), (), s32[]{:S(2)}) async-start(), calls=%async_computation.23 | async-start | bytes 1310720 | tf_op jit(solution)/shard_map/reduce_scatter | solution.py:324
  707.8 140.7 %reduce-scatter.11.cloned.1.call-start = ((), (), s32[]{:S(2)}) async-start(), calls=%async_computation.17 | async-start | bytes 983040 | tf_op jit(solution)/shard_map/reduce_scatter | solution.py:297
  730.6 7.5 copy-start.30
  738.1 32.6 %copy-start.33 = (bf16[1024]{0:T(1024)(128)(2,1)S(1)}, bf16[1024]{0:T(1024)(128)(2,1)}, u32[]{:S(2)}) copy-start(bf16[1024]{0:T(1024)(128)(2,1)} %get-tuple-element.234) | copy-start | bytes 6148
  738.1 32.6 %copy-start.34 = (bf16[1024]{0:T(1024)(128)(2,1)S(1)}, bf16[1024]{0:T(1024)(128)(2,1)}, u32[]{:S(2)}) copy-start(bf16[1024]{0:T(1024)(128)(2,1)} %get-tuple-element.247) | copy-start | bytes 6148
  738.1 32.6 %copy-start.35 = (bf16[4096]{0:T(1024)(128)(2,1)S(1)}, bf16[4096]{0:T(1024)(128)(2,1)}, u32[]{:S(2)}) copy-start(bf16[4096]{0:T(1024)(128)(2,1)} %get-tuple-element.253) | copy-start | bytes 24580
  738.1 32.6 %copy-start.40 = (bf16[1024]{0:T(1024)(128)(2,1)S(1)}, bf16[1024]{0:T(1024)(128)(2,1)}, u32[]{:S(2)}) copy-start(bf16[1024]{0:T(1024)(128)(2,1)} %get-tuple-element.165) | copy-start | bytes 6148
  738.1 32.6 %copy-start.41 = (bf16[1024]{0:T(1024)(128)(2,1)S(1)}, bf16[1024]{0:T(1024)(128)(2,1)}, u32[]{:S(2)}) copy-start(bf16[1024]{0:T(1024)(128)(2,1)} %get-tuple-element.171) | copy-start | bytes 6148
  738.1 72.5 %copy-start.10 = (f32[384,1024]{1,0:T(8,128)S(1)}, f32[384,1024]{1,0:T(8,128)}, u32[]{:S(2)}) copy-start(f32[384,1024]{1,0:T(8,128)} %copy-done.9) | copy-start | bytes 4718596
  738.1 72.5 %copy-start.16 = (bf16[384,1024]{1,0:T(8,128)(2,1)S(1)}, bf16[384,1024]{1,0:T(8,128)(2,1)}, u32[]{:S(2)}) copy-start(bf16[384,1024]{1,0:T(8,128)(2,1)} %param.35) | copy-start | bytes 2359300
  738.1 72.5 %copy-start.28 = (f32[384]{0:T(512)S(1)}, f32[384]{0:T(512)}, u32[]{:S(2)}) copy-start(f32[384]{0:T(512)} %copy-done.27) | copy-start | bytes 4612
  (12 other events, 21.2 us)
Sparse Core Ops, SparseCore 0:
  9.9 48.2 all-gather.14
  60.1 27.8 all-gather.16
  89.9 54.3 all-gather.18
  146.1 54.3 all-gather.20
  342.7 41.5 reduce-scatter.12
  388.1 71.2 reduce-scatter.16
  462.8 71.2 reduce-scatter.20
  623.8 27.1 reduce-scatter.14
  706.6 60.0 reduce-scatter.8
  769.0 27.1 reduce-scatter.18
  798.5 25.8 reduce-scatter.22
  826.6 21.8 reduce-scatter.10
where the time goes:
time: 865 us; the launch traced here: 857 us
  matrix products  265 us (31%)
  blocking collectives  190 us (22%)
  waiting for transfers between devices  160 us (18%)
  local copies, waits for them, and re-layouts  110 us (13%)
  other arithmetic  83 us (10%)
  starting transfers between devices  18.2 us (2%)
  between operations  17.8 us (2%)
  loops' own time  13.6 us (2%)
    all_gather x1, blocking collectives, shards(): span_labels = lax.all_gather(segment_ids, 'seq', axis=0, tiled=True)  75.7 us
    all_to_all x1, waiting for transfers between devices, shards(): lax.all_to_all(head_grads, 'seq', split_axis=0, concat_axis=2, tiled=True)  74.2 us
    dot_general x4, matrix products, block_scores(): jnp.einsum('qhd,khd->hqk', query_block, key_window, preferred_element_typ...  50.2 us
    dot_general x2, matrix products, block_backward(): jnp.einsum('qhd,khd->hqk', grad_block, value_window, preferred_element_ty...  44.4 us
    dynamic_update_slice x4, local copies, waits for them, and re-layouts, add_window(): return lax.dynamic_update_slice_in_dim(total, current + delta, start, 0)  39.2 us
    unnamed x2, blocking collectives  36.3 us
    convert_element_type x2, other arithmetic, block_backward(): grad_scores = (probs_full * (grad_probs - row_inner)).astype(jnp.bfloat16)  34.8 us
    dot_general x4, matrix products, contract_rows(): lax.dot_general(left, right, (((0,), (0,)), ((), ())), preferred_element_...  30.1 us
  transfers between devices with their start and end apart: 16, of which 6 were waited for; matrix products, arithmetic and copies ran while one was open for 49% of the time, Pallas kernels for 0%

commit v1 on v0

--- a/solution.py
+++ b/solution.py
@@ -8,6 +8,22 @@
 LEN = 577
 norm_eps = 1e-06
 masked_score = -1000000000.0
+
+
+def swapped_with_each(x, axis, split, join):
+    ways, here = (lax.axis_size(axis), lax.axis_index(axis))
+    width = x.shape[split] // ways
+    lengths = list(x.shape)
+    lengths[split] = width
+    height = lengths[join]
+    lengths[join] = height * ways
+    full = jnp.zeros(lengths, x.dtype)
+    for mask in range(ways):
+        part = lax.dynamic_slice_in_dim(x, (here ^ mask) * width, width, axis=split)
+        if mask:
+            part = lax.ppermute(part, axis, [(d, d ^ mask) for d in range(ways)])
+        full = lax.dynamic_update_slice_in_dim(full, part, (here ^ mask) * height, axis=join)
+    return full
 
 
 def normalize(values, gain, shift):
@@ -185,9 +201,7 @@
     out_bias_part = column_sum(grad_mixed)
     w_out_part = weight_grad(attended, grad_mixed)
     grad_attended = times_transposed(grad_mixed, attn_set[5]).astype(jnp.bfloat16)
-    grad_heads = lax.all_to_all(
-        grad_attended, "seq", split_axis=1, concat_axis=0, tiled=True
-    ).reshape(span_rows, local_heads, HD)
+    grad_heads = swapped_with_each(grad_attended, "seq", 1, 0).reshape(span_rows, local_heads, HD)
 
     def block_backward(running, inputs_block):
         key_total, value_total = running

time: 865 us -> 856 us (0.990)
    all_to_all x1 -> x0, waiting for transfers between devices: 10.6 us -> none  [shards(): lax.all_to_all(grad_attended, 'seq', split_axis=1, concat_axis=0, tiled=T...]
  transfers between devices with their start and end apart: 16 -> 18, of which waited for: 6 -> 6; matrix products, arithmetic and copies ran while one was open for 49% -> 49% of each run, Pallas kernels for 0% -> 0%
where the time goes in v1:
time: 856 us; the launch traced here: 849 us
  matrix products  261 us (30%)
  blocking collectives  189 us (22%)
  waiting for transfers between devices  155 us (18%)
  local copies, waits for them, and re-layouts  111 us (13%)
  other arithmetic  82.6 us (10%)
  starting transfers between devices  18.1 us (2%)
  between operations  17.8 us (2%)
  loops' own time  13.6 us (2%)
    all_gather x1, blocking collectives, shards(): span_labels = lax.all_gather(segment_ids, 'seq', axis=0, tiled=True)  75.7 us
    all_to_all x1, waiting for transfers between devices, shards(): lax.all_to_all(head_grads, 'seq', split_axis=0, concat_axis=2, tiled=True)  72.7 us
    dot_general x4, matrix products, block_scores(): jnp.einsum('qhd,khd->hqk', query_block, key_window, preferred_element_typ...  51.7 us
    dot_general x2, matrix products, block_backward(): jnp.einsum('qhd,khd->hqk', grad_block, value_window, preferred_element_ty...  44.3 us
    dynamic_update_slice x4, local copies, waits for them, and re-layouts, add_window(): return lax.dynamic_update_slice_in_dim(total, current + delta, start, 0)  39.3 us
    unnamed x2, blocking collectives  36.3 us
    convert_element_type x2, other arithmetic, block_backward(): grad_scores = (probs_full * (grad_probs - row_inner)).astype(jnp.bfloat16)  34.4 us
    reduce_scatter x1, waiting for transfers between devices, shards(): lax.psum_scatter(w_qkv_part.astype(jnp.bfloat16), 'fsdp', scatter_dimensi...  28.3 us
  transfers between devices with their start and end apart: 18, of which 6 were waited for; matrix products, arithmetic and copies ran while one was open for 49% of the time, Pallas kernels for 0%

profile of v1, /device:TPU:0, one launch (start us, length us, event | category | flops | bytes accessed | tf_op | source)
XLA Modules:
  0.0 848.6 jit_solution(2262013457316206588)
XLA Ops:
  9.4 10.3 %all-gather.3 = bf16[8,1,128]{2,1,0:T(2,128)(2,1)S(1)} all-gather(bf16[1,1,128]{2,1,0:T(2,128)(2,1)} %bitcast.138), channel_id=1, replica_groups=mesh['fsdp'=8,'seq'=4] {'fsdp'}, dimensions={0}, use_global_device_ids=true | all-gather | bytes 2304 | tf_op jit(solution)/shard_map/all_gather | solution.py:103
  19.7 8.6 %all-gather.2 = bf16[8,1,128]{2,1,0:T(2,128)(2,1)S(1)} all-gather(bf16[1,1,128]{2,1,0:T(2,128)(2,1)} %bitcast.139), channel_id=1, replica_groups=mesh['fsdp'=8,'seq'=4] {'fsdp'}, dimensions={0}, use_global_device_ids=true | all-gather | bytes 2304 | tf_op jit(solution)/shard_map/all_gather | solution.py:102
  28.3 7.9 all-gather.1
  36.2 8.6 %all-gather = bf16[8,1,128]{2,1,0:T(2,128)(2,1)S(1)} all-gather(bf16[1,1,128]{2,1,0:T(2,128)(2,1)} %bitcast.141), channel_id=1, replica_groups=mesh['fsdp'=8,'seq'=4] {'fsdp'}, dimensions={0}, use_global_device_ids=true | all-gather | bytes 2304 | tf_op jit(solution)/shard_map/all_gather | solution.py:99
  47.1 11.1 %all-gather.15.cloned.1.call-done = bf16[1024,3072]{1,0:T(8,128)(2,1)} async-done(((bf16[128,3072]{1,0:T(8,128)(2,1)}), bf16[1024,3072]{1,0:T(8,128)(2,1)}) %all-gather.15.cloned.1.call-update) | async-done | bytes 6291472 | tf_op jit(solution)/shard_map/all_gather | solution.py:101
  58.2 6.9 add_convert_fusion.1
  65.1 3.0 copy.77
  68.1 3.7 copy.78
  71.8 4.7 all-to-all-start
  77.1 75.7 %all-gather.4 = s32[4,1,384]{2,1,0:T(1,128)S(1)} all-gather(s32[1,1,384]{2,1,0:T(1,128)S(1)} %reshape.220), channel_id=1, replica_groups=mesh['fsdp'=8,'seq'=4] {'seq'}, dimensions={0}, use_global_device_ids=true | all-gather | bytes 7680 | tf_op jit(solution)/shard_map/all_gather | solution.py:107
  154.7 3.0 copy.80
  165.7 80.9 %while.26 = (s32[]{:T(128)}, bf16[2,768,4,64]{1,3,2,0:T(8,128)(2,1)}, f32[2,4,768]{2,1,0:T(4,128)S(1)}, s32[2]{0:T(128)S(1)}, bf16[2688,4,64]{0,2,1:T(8,128)(2,1...) while((s32[]{:T(128)}, ...), condition=%wide.region_5.6_spmd, body=%wide.region_2.5_spmd.sunk | while | flops 1582396416 | bytes 85851936 | solution.py:158
  170.6 11.8 %fusion.119 = (f32[4,768]{1,0:T(4,128)S(1)}, f32[4,768,1920]{2,1,0:T(8,128)}) fusion(pred[768,1920]{1,0:T(8,128)(4,1)S(1)} %broadcast_compare_fusion.4, bf16[2688,4,64]{0,2,1:T(8,128)(2,1)S(1)} %get-tuple-element.425, s32[]{:T(128)S(6)} %select_n.103, bf16[1536,4,64]{0,2,1:T(8,128)(2,1)} %get-tuple-element.424, s32[]{:T(128)S(6)} %select_n.104), kind=kOutput, calls=%fused_computation.3.clone.1 | convolution fusion | flops 772666368 | bytes 26456072 | tf_op jit(solution)/shard_map/while/body/eval_jaxpr/qhd,khd->hqk/dot_general | solution.py:136
  182.5 11.2 %fusion.120 = f32[4,768]{1,0:T(4,128)S(1)} fusion(f32[4,768,1920]{2,1,0:T(8,128)} %get-tuple-element.375, f32[4,768]{1,0:T(4,128)S(1)} %get-tuple-element.376, pred[768,1920]{1,0:T(8,128)(4,1)S(1)} %broadcast_compare_fusion.4), kind=kLoop, calls=%fused_computation.4.clone.1 | loop fusion | flops 23589888 | bytes 25092096 | tf_op jit(solution)/shard_map/while/body/eval_jaxpr/reduce_sum | solution.py:151
  193.7 11.7 %fusion.121 = bf16[2,768,4,64]{1,3,2,0:T(8,128)(2,1)S(1)} fusion(bf16[2,768,4,64]{1,3,2,0:T(8,128)(2,1)S(1)} %copy-done.19, s32[]{:T(128)S(6)} %copy.100, f32[4,768,1920]{2,1,0:T(8,128)} %get-tuple-element.375, f32[4,768]{1,0:T(4,128)S(1)} %fusion.120, f32[4,768]{1,0:T(4,128)S(1)} %get-tuple-element.376, ...), kind=kOutput, calls=%fused_computation.9.clone.1 | convolution fusion | flops 784662528 | bytes 26468360 | tf_op jit(solution)/shard_map/while/body/eval_jaxpr/hqk,khd->qhd/dot_general | solution.py:153
  211.1 11.8 %fusion.119 = (f32[4,768]{1,0:T(4,128)S(1)}, f32[4,768,1920]{2,1,0:T(8,128)}) fusion(pred[768,1920]{1,0:T(8,128)(4,1)S(1)} %broadcast_compare_fusion.4, bf16[2688,4,64]{0,2,1:T(8,128)(2,1)S(1)} %get-tuple-element.425, s32[]{:T(128)S(6)} %select_n.103, bf16[1536,4,64]{0,2,1:T(8,128)(2,1)} %get-tuple-element.424, s32[]{:T(128)S(6)} %select_n.104), kind=kOutput, calls=%fused_computation.3.clone.1 | convolution fusion | flops 772666368 | bytes 26456072 | tf_op jit(solution)/shard_map/while/body/eval_jaxpr/qhd,khd->hqk/dot_general | solution.py:136
  222.9 11.1 %fusion.120 = f32[4,768]{1,0:T(4,128)S(1)} fusion(f32[4,768,1920]{2,1,0:T(8,128)} %get-tuple-element.375, f32[4,768]{1,0:T(4,128)S(1)} %get-tuple-element.376, pred[768,1920]{1,0:T(8,128)(4,1)S(1)} %broadcast_compare_fusion.4), kind=kLoop, calls=%fused_computation.4.clone.1 | loop fusion | flops 23589888 | bytes 25092096 | tf_op jit(solution)/shard_map/while/body/eval_jaxpr/reduce_sum | solution.py:151
  234.0 11.7 %fusion.121 = bf16[2,768,4,64]{1,3,2,0:T(8,128)(2,1)S(1)} fusion(bf16[2,768,4,64]{1,3,2,0:T(8,128)(2,1)S(1)} %copy-done.19, s32[]{:T(128)S(6)} %copy.100, f32[4,768,1920]{2,1,0:T(8,128)} %get-tuple-element.375, f32[4,768]{1,0:T(4,128)S(1)} %fusion.120, f32[4,768]{1,0:T(4,128)S(1)} %get-tuple-element.376, ...), kind=kOutput, calls=%fused_computation.9.clone.1 | convolution fusion | flops 784662528 | bytes 26468360 | tf_op jit(solution)/shard_map/while/body/eval_jaxpr/hqk,khd->qhd/dot_general | solution.py:153
  249.5 3.3 all_to_all.42
  254.9 4.4 all-to-all-start.1
  259.4 9.1 %all-gather.5 = bf16[8,1,128]{2,1,0:T(2,128)(2,1)S(1)} all-gather(bf16[1,1,128]{2,1,0:T(2,128)(2,1)S(1)} %bitcast.142), channel_id=1, replica_groups=mesh['fsdp'=8,'seq'=4] {'fsdp'}, dimensions={0}, use_global_device_ids=true | all-gather | bytes 2304 | tf_op jit(solution)/shard_map/all_gather | solution.py:105
  268.5 8.3 all-gather.8
  276.9 8.4 all-gather.7
  285.2 8.1 all-gather.6
  293.4 3.1 fusion.80
  298.0 21.1 %multiply_convert_fusion.1 = (bf16[384,4096]{1,0:T(8,128)(2,1)}, f32[384,4096]{1,0:T(8,128)}, f32[384,4096]{1,0:T(8,128)}) fusion(f32[4096]{0:T(1024)S(1)} %bitcast.126, bf16[1024,4096]{1,0:T(8,128)(2,1)} %all-gather.19.cloned.1.call-done, f32[384,1024]{1,0:T(8,128)} %copy-done.11, f32[1024]{0:T(1024)S(1)} %bitcast.135, f32[1024]{0:T(1024)S(1)} %bitcast.129, ...), kind=kOutput, calls=%fused_computation.56 | convolution fusion | flops 3327000576 | bytes 25717760 | tf_op jit(solution)/shard_map/dot_general | solution.py:176
  319.1 11.7 %fusion.81 = (bf16[4096]{0:T(1024)(128)(2,1)}, bf16[384,4096]{1,0:T(8,128)(2,1)S(1)}) fusion(f32[384,4096]{1,0:T(8,128)} %get-tuple-element.227, f32[384,4096]{1,0:T(8,128)} %get-tuple-element.242, bf16[4096,1024]{1,0:T(8,128)(2,1)} %all-gather.21.cloned.1.call-done, bf16[384,1024]{1,0:T(8,128)(2,1)} %param.35, f32[384]{0:T(512)S(1)} %compare_convert_fusion), kind=kOutput, calls=%fused_computation.143 | convolution fusion | flops 3245993984 | bytes 24913408 | tf_op jit(solution)/shard_map/dot_general | solution.py:43
  330.8 4.3 multiply_reduce_fusion.1
  338.8 3.7 convolution_convert_fusion.3
  342.6 10.4 %convolution_convert_fusion.1 = bf16[1024,4096]{1,0:T(8,128)(2,1)} fusion(bf16[384,4096]{1,0:T(8,128)(2,1)} %copy-done.51, f32[384,1024]{1,0:T(8,128)} %copy-done.11, f32[1024]{0:T(1024)S(1)} %bitcast.136, f32[1024]{0:T(1024)S(1)} %bitcast.132, f32[384]{0:T(512)S(1)} %fusion.64, f32[384]{0:T(512)S(1)} %broadcast_multiply_fusion), kind=kOutput, calls=%fused_computation.53 | convolution fusion | flops 3227385856 | bytes 13118464 | tf_op jit(solution)/shard_map/dot_general | solution.py:37
  353.1 3.1 convolution_convert_fusion.4
  362.5 7.1 convolution_convert_fusion
  370.4 7.0 collective-permute-done.1
  384.8 213.3 %while.27 = (s32[]{:T(128)}, f32[2688,4,64]{0,2,1:T(8,128)}, f32[2688,4,64]{0,2,1:T(8,128)}, bf16[2,768,4,64]{1,3,2,0:T(8,128)(2,1)}, s32[2]{0:T(128)S(1)}, /*in...) while((s32[]{:T(128)}, f32[2688,4,64]{0,2,1:T(8,128)}, ...), condition=%wide.region_12.13_spmd, body=%wide.region_10.12_spmd.sunk | while | flops 3866489856 | bytes 287363040 | solution.py:238
  388.9 15.7 %fusion.130 = f32[4,768,1920]{2,1,0:T(8,128)} fusion(bf16[2688,4,64]{0,2,1:T(8,128)(2,1)S(1)} %get-tuple-element.470, s32[]{:T(128)S(6)} %select_n.108, bf16[1536,4,64]{0,2,1:T(8,128)(2,1)} %get-tuple-element.467, s32[]{:T(128)S(6)} %select_n.109), kind=kOutput, calls=%fused_computation.37.clone.1 | convolution fusion | flops 754974720 | bytes 24969224 | tf_op jit(solution)/shard_map/while/body/eval_jaxpr/qhd,khd->hqk/dot_general | solution.py:136
  405.7 22.2 %multiply_reduce_fusion.5 = (f32[4,768]{1,0:T(4,128)S(1)}, f32[4,768,1920]{2,1,0:T(8,128)}) fusion(f32[4,768,1920]{2,1,0:T(8,128)} %fusion.130, f32[4,768]{1,0:T(4,128)S(1)} %dynamic-slice_bitcast_fusion.2, pred[768,1920]{1,0:T(8,128)(4,1)S(1)} %broadcast_compare_fusion.5, bf16[2688,4,64]{0,2,1:T(8,128)(2,1)S(1)} %get-tuple-element.473, ...), kind=kOutput, calls=%fused_computation.20.clone.1 | convolution fusion | flops 784462848 | bytes 50061320 | tf_op jit(solution)/shard_map/while/body/eval_jaxpr/qhd,khd->hqk/dot_general | solution.py:216
  427.9 17.4 %multiply_convert_fusion.4 = bf16[4,768,1920]{2,1,0:T(8,128)(2,1)S(1)} fusion(f32[4,768,1920]{2,1,0:T(8,128)} %get-tuple-element.389, f32[4,768,1920]{2,1,0:T(8,128)} %fusion.130, f32[4,768]{1,0:T(4,128)S(1)} %get-tuple-element.390, f32[4,768]{1,0:T(4,128)S(1)} %dynamic-slice_bitcast_fusion.2, pred[768,1920]{1,0:T(8,128)(4,1)S(1)} %broadcast_compare_fusion.5), kind=kLoop, calls=%fused_computation.19.clone.1 | loop fusion | flops 35389440 | bytes 60481536 | tf_op jit(solution)/shard_map/while/body/eval_jaxpr/convert_element_type | solution.py:220
  445.3 4.3 copy-done
  451.5 10.0 %dynamic_update_slice.49 = f32[2688,4,64]{0,2,1:T(8,128)} dynamic-update-slice(f32[2688,4,64]{0,2,1:T(8,128)} %get-tuple-element.447, f32[1920,4,64]{0,2,1:T(8,128)S(1)} %fusion.131, s32[]{:T(128)S(6)} %select_n.108, s32[]{:T(128)} %constant.80.clone.1..sunk.1, s32[]{:T(128)} %constant.80.clone.1..sunk.1) | dynamic-update-slice | bytes 3932164 | tf_op jit(solution)/shard_map/while/body/eval_jaxpr/dynamic_update_slice | solution.py:61
  461.6 13.2 %fusion.132 = f32[1920,4,64]{0,2,1:T(8,128)S(1)} fusion(f32[4,768,1920]{2,1,0:T(8,128)} %fusion.130, f32[4,768]{1,0:T(4,128)S(1)} %dynamic-slice_bitcast_fusion.2, pred[768,1920]{1,0:T(8,128)(4,1)S(1)} %broadcast_compare_fusion.5, f32[2688,4,64]{0,2,1:T(8,128)} %get-tuple-element.448, s32[]{:T(128)S(6)} %select_n.108, ...), kind=kOutput, calls=%fused_computation.30.clone.1 | convolution fusion | flops 779059200 | bytes 29405192 | tf_op jit(solution)/shard_map/while/body/eval_jaxpr/hqk,qhd->khd/dot_general | solution.py:213
  474.7 10.3 %dynamic_update_slice.50 = f32[2688,4,64]{0,2,1:T(8,128)} dynamic-update-slice(f32[2688,4,64]{0,2,1:T(8,128)} %get-tuple-element.448, f32[1920,4,64]{0,2,1:T(8,128)S(1)} %fusion.132, s32[]{:T(128)S(6)} %select_n.108, s32[]{:T(128)} %constant.80.clone.1..sunk.1, s32[]{:T(128)} %constant.80.clone.1..sunk.1) | dynamic-update-slice | bytes 3932164 | tf_op jit(solution)/shard_map/while/body/eval_jaxpr/dynamic_update_slice | solution.py:61
  485.1 9.6 %fusion.133 = bf16[2,768,4,64]{1,3,2,0:T(8,128)(2,1)} fusion(bf16[2,768,4,64]{1,3,2,0:T(8,128)(2,1)} %get-tuple-element.449, s32[]{:T(128)S(6)} %copy.114, bf16[4,768,1920]{2,1,0:T(8,128)(2,1)} %copy-done, bf16[2688,4,64]{0,2,1:T(8,128)(2,1)S(1)} %copy-done.2, s32[]{:T(128)S(6)} %select_n.108), kind=kOutput, calls=%fused_computation.33.clone.1 | convolution fusion | flops 755171328 | bytes 13565960 | tf_op jit(solution)/shard_map/while/body/eval_jaxpr/hqk,khd->qhd/dot_general | solution.py:222
  498.6 12.4 %fusion.130 = f32[4,768,1920]{2,1,0:T(8,128)} fusion(bf16[2688,4,64]{0,2,1:T(8,128)(2,1)S(1)} %get-tuple-element.470, s32[]{:T(128)S(6)} %select_n.108, bf16[1536,4,64]{0,2,1:T(8,128)(2,1)} %get-tuple-element.467, s32[]{:T(128)S(6)} %select_n.109), kind=kOutput, calls=%fused_computation.37.clone.1 | convolution fusion | flops 754974720 | bytes 24969224 | tf_op jit(solution)/shard_map/while/body/eval_jaxpr/qhd,khd->hqk/dot_general | solution.py:136
  512.1 22.1 %multiply_reduce_fusion.5 = (f32[4,768]{1,0:T(4,128)S(1)}, f32[4,768,1920]{2,1,0:T(8,128)}) fusion(f32[4,768,1920]{2,1,0:T(8,128)} %fusion.130, f32[4,768]{1,0:T(4,128)S(1)} %dynamic-slice_bitcast_fusion.2, pred[768,1920]{1,0:T(8,128)(4,1)S(1)} %broadcast_compare_fusion.5, bf16[2688,4,64]{0,2,1:T(8,128)(2,1)S(1)} %get-tuple-element.473, ...), kind=kOutput, calls=%fused_computation.20.clone.1 | convolution fusion | flops 784462848 | bytes 50061320 | tf_op jit(solution)/shard_map/while/body/eval_jaxpr/qhd,khd->hqk/dot_general | solution.py:216
  534.3 17.0 %multiply_convert_fusion.4 = bf16[4,768,1920]{2,1,0:T(8,128)(2,1)S(1)} fusion(f32[4,768,1920]{2,1,0:T(8,128)} %get-tuple-element.389, f32[4,768,1920]{2,1,0:T(8,128)} %fusion.130, f32[4,768]{1,0:T(4,128)S(1)} %get-tuple-element.390, f32[4,768]{1,0:T(4,128)S(1)} %dynamic-slice_bitcast_fusion.2, pred[768,1920]{1,0:T(8,128)(4,1)S(1)} %broadcast_compare_fusion.5), kind=kLoop, calls=%fused_computation.19.clone.1 | loop fusion | flops 35389440 | bytes 60481536 | tf_op jit(solution)/shard_map/while/body/eval_jaxpr/convert_element_type | solution.py:220
  551.3 4.3 copy-done
  557.7 9.4 %dynamic_update_slice.49 = f32[2688,4,64]{0,2,1:T(8,128)} dynamic-update-slice(f32[2688,4,64]{0,2,1:T(8,128)} %get-tuple-element.447, f32[1920,4,64]{0,2,1:T(8,128)S(1)} %fusion.131, s32[]{:T(128)S(6)} %select_n.108, s32[]{:T(128)} %constant.80.clone.1..sunk.1, s32[]{:T(128)} %constant.80.clone.1..sunk.1) | dynamic-update-slice | bytes 3932164 | tf_op jit(solution)/shard_map/while/body/eval_jaxpr/dynamic_update_slice | solution.py:61
  567.1 12.4 %fusion.132 = f32[1920,4,64]{0,2,1:T(8,128)S(1)} fusion(f32[4,768,1920]{2,1,0:T(8,128)} %fusion.130, f32[4,768]{1,0:T(4,128)S(1)} %dynamic-slice_bitcast_fusion.2, pred[768,1920]{1,0:T(8,128)(4,1)S(1)} %broadcast_compare_fusion.5, f32[2688,4,64]{0,2,1:T(8,128)} %get-tuple-element.448, s32[]{:T(128)S(6)} %select_n.108, ...), kind=kOutput, calls=%fused_computation.30.clone.1 | convolution fusion | flops 779059200 | bytes 29405192 | tf_op jit(solution)/shard_map/while/body/eval_jaxpr/hqk,qhd->khd/dot_general | solution.py:213
  579.5 9.5 %dynamic_update_slice.50 = f32[2688,4,64]{0,2,1:T(8,128)} dynamic-update-slice(f32[2688,4,64]{0,2,1:T(8,128)} %get-tuple-element.448, f32[1920,4,64]{0,2,1:T(8,128)S(1)} %fusion.132, s32[]{:T(128)S(6)} %select_n.108, s32[]{:T(128)} %constant.80.clone.1..sunk.1, s32[]{:T(128)} %constant.80.clone.1..sunk.1) | dynamic-update-slice | bytes 3932164 | tf_op jit(solution)/shard_map/while/body/eval_jaxpr/dynamic_update_slice | solution.py:61
  589.0 8.9 %fusion.133 = bf16[2,768,4,64]{1,3,2,0:T(8,128)(2,1)} fusion(bf16[2,768,4,64]{1,3,2,0:T(8,128)(2,1)} %get-tuple-element.449, s32[]{:T(128)S(6)} %copy.114, bf16[4,768,1920]{2,1,0:T(8,128)(2,1)} %copy-done, bf16[2688,4,64]{0,2,1:T(8,128)(2,1)S(1)} %copy-done.2, s32[]{:T(128)S(6)} %select_n.108), kind=kOutput, calls=%fused_computation.33.clone.1 | convolution fusion | flops 755171328 | bytes 13565960 | tf_op jit(solution)/shard_map/while/body/eval_jaxpr/hqk,khd->qhd/dot_general | solution.py:222
  606.4 3.6 copy.89
  610.0 4.2 all-to-all-start.2
  615.0 72.7 %all-to-all-done.2 = bf16[1536,3,256]{2,1,0:T(4,128)(2,1)S(1)} async-done(((bf16[1536,3,256]{2,1,0:T(4,128)(2,1)}), bf16[1536,3,256]{2,1,0:T(4,128)(2,1)S(1)}, u32[]{:S(2)}, u32[]{:S(2)}) %all-to-all-start.2) | async-done | bytes 2359328 | tf_op jit(solution)/shard_map/all_to_all | solution.py:251
  689.4 3.1 copy.91
  692.5 5.9 convolution_convert_fusion.2
  699.9 8.1 all-gather.9
  711.8 8.7 %multiply_convert_fusion.2 = bf16[384,1024]{1,0:T(8,128)(2,1)} fusion(f32[384,1024]{1,0:T(8,128)S(1)} %copy-done.13, bf16[384,4096]{1,0:T(8,128)(2,1)} %get-tuple-element.226, bf16[4096,1024]{1,0:T(8,128)(2,1)} %all-gather.21.cloned.1.call-done, f32[1024]{0:T(1024)S(1)} %bitcast.137, f32[384]{0:T(512)S(1)} %copy-done.27), kind=kOutput, calls=%fused_computation.99 | convolution fusion | flops 3222798336 | bytes 13899264 | tf_op jit(solution)/shard_map/dot_general | solution.py:180
  722.1 7.4 fusion.74
  729.6 28.3 %reduce-scatter.9.cloned.1.call-done = bf16[128,3072]{1,0:T(8,128)(2,1)} async-done(((bf16[1024,3072]{1,0:T(8,128)(2,1)}), bf16[128,3072]{1,0:T(8,128)(2,1)}) %reduce-scatter.9.cloned.1.call-update) | async-done | bytes 786448 | tf_op jit(solution)/shard_map/reduce_scatter | solution.py:270
  761.8 23.8 %all-reduce.21 = (bf16[1024]{0:T(1024)(128)(2,1)S(1)}, bf16[1024]{0:T(1024)(128)(2,1)S(1)}, bf16[1024]{0:T(1024)(128)(2,1)S(1)}, bf16[1024]{0:T(1024)(128)(2,1)S...) all-reduce(bf16[1024]{0:T(1024)(128)(2,1)S(1)} %get-tuple-element.1, ...), channel_id=2, replica_groups=mesh['fsdp'=8,'seq'=4] {'fsdp'}, use_global_device_ids=true, to_apply=%region_16.17.clone | all-reduce | flops 12288 | bytes 49152
  786.3 12.5 %all-reduce.22 = (bf16[128]{0:T(256)(128)(2,1)S(1)}, bf16[128]{0:T(256)(128)(2,1)S(1)}, bf16[128]{0:T(256)(128)(2,1)S(1)}, bf16[128]{0:T(256)(128)(2,1)S(1)}, bf...) all-reduce(bf16[128]{0:T(256)(128)(2,1)S(1)} %dynamic-slice.1, ...), channel_id=3, replica_groups=mesh['fsdp'=8,'seq'=4] {'seq'}, use_global_device_ids=true, to_apply=%region_17.18.clone | all-reduce | flops 1536 | bytes 6144
  801.8 3.3 add_add_fusion.2
  806.9 8.6 %reduce-scatter.23.cloned.1.call-done = bf16[512,256]{1,0:T(8,128)(2,1)} async-done(((bf16[512,1024]{1,0:T(8,128)(2,1)}), bf16[512,256]{1,0:T(8,128)(2,1)}) %reduce-scatter.23.cloned.1.call-update) | async-done | bytes 262160 | tf_op jit(solution)/shard_map/reduce_scatter | solution.py:338
  817.3 22.4 %reduce-scatter.11.cloned.1.call-done = bf16[128,768]{1,0:T(8,128)(2,1)} async-done(((bf16[128,3072]{1,0:T(8,128)(2,1)}), bf16[128,768]{1,0:T(8,128)(2,1)}) %reduce-scatter.11.cloned.1.call-update) | async-done | bytes 196624 | tf_op jit(solution)/shard_map/reduce_scatter | solution.py:311
  (263 shorter events, 79.7 us)
Async XLA Ops:
  7.2 39.0 %copy-start.7 = (bf16[384,1024]{1,0:T(8,128)(2,1)S(1)}, bf16[384,1024]{1,0:T(8,128)(2,1)}, u32[]{:S(2)}) copy-start(bf16[384,1024]{1,0:T(8,128)(2,1)} %param.20) | copy-start | bytes 2359300
  7.2 51.0 %all-gather.15.cloned.1.call-start = ((), (), s32[]{:S(2)}) async-start(), calls=%async_computation.11 | async-start | bytes 7077888 | tf_op jit(solution)/shard_map/all_gather | solution.py:101
  7.9 285.5 %all-gather.17.cloned.1.call-start = ((), (), s32[]{:S(2)}) async-start(), calls=%async_computation.12 | async-start | bytes 2359296 | tf_op jit(solution)/shard_map/all_gather | solution.py:104
  8.7 289.3 %all-gather.19.cloned.1.call-start = ((), (), s32[]{:S(2)}) async-start(), calls=%async_computation.13 | async-start | bytes 9437184 | tf_op jit(solution)/shard_map/all_gather | solution.py:168
  36.2 22.0 %copy-start.39 = (f32[8,1,128]{2,1,0:T(1,128)}, f32[8,1,128]{2,1,0:T(1,128)S(1)}, u32[]{:S(2)}) copy-start(f32[8,1,128]{2,1,0:T(1,128)S(1)} %convert_element_type.226) | copy-start | bytes 12292
  44.8 13.4 %copy-start.22 = (f32[8,1,128]{2,1,0:T(1,128)}, f32[8,1,128]{2,1,0:T(1,128)S(1)}, u32[]{:S(2)}) copy-start(f32[8,1,128]{2,1,0:T(1,128)S(1)} %convert_element_type.225) | copy-start | bytes 12292
  46.2 12.0 %copy-start.24 = (f32[384]{0:T(512)}, f32[384]{0:T(512)S(1)}, u32[]{:S(2)}) copy-start(f32[384]{0:T(512)S(1)} %broadcast_multiply_fusion.1) | copy-start | bytes 4612
  47.1 11.1 %copy-start.32 = (f32[384]{0:T(512)}, f32[384]{0:T(512)S(1)}, u32[]{:S(2)}) copy-start(f32[384]{0:T(512)S(1)} %fusion.63) | copy-start | bytes 4612
  71.8 5.3 copy-start.37
  71.8 81.2 %all-to-all-start = ((bf16[384,3,1024]{0,1,2:T(4,128)(2,1)}), bf16[384,3,1024]{0,1,2:T(4,128)(2,1)S(1)}, u32[]{:S(2)}, u32[]{:S(2)}) async-start(bf16[384,3,1024]{0,1,2:T(4,128)(2,1)} %copy.78), calls=%async_computation | async-start | bytes 6291456 | tf_op jit(solution)/shard_map/all_to_all | solution.py:121
  76.5 242.6 %all-gather.21.cloned.1.call-start = ((), (), s32[]{:S(2)}) async-start(), calls=%async_computation.14 | async-start | bytes 9437184 | tf_op jit(solution)/shard_map/all_gather | solution.py:170
  182.5 11.2 %copy-start.19 = (bf16[2,768,4,64]{1,3,2,0:T(8,128)(2,1)S(1)}, bf16[2,768,4,64]{1,3,2,0:T(8,128)(2,1)}, u32[]{:S(2)}) copy-start(bf16[2,768,4,64]{1,3,2,0:T(8,128)(2,1)} %get-tuple-element.405) | copy-start | bytes 2359300 | tf_op jit(solution)/shard_map/while
  222.9 11.1 %copy-start.19 = (bf16[2,768,4,64]{1,3,2,0:T(8,128)(2,1)S(1)}, bf16[2,768,4,64]{1,3,2,0:T(8,128)(2,1)}, u32[]{:S(2)}) copy-start(bf16[2,768,4,64]{1,3,2,0:T(8,128)(2,1)} %get-tuple-element.405) | copy-start | bytes 2359300 | tf_op jit(solution)/shard_map/while
  246.6 12.8 %copy-start.44 = (bf16[128]{0:T(256)(128)(2,1)S(1)}, bf16[128]{0:T(256)(128)(2,1)}, u32[]{:S(2)}) copy-start(bf16[128]{0:T(256)(128)(2,1)} %param.28) | copy-start | bytes 772
  246.6 21.9 %copy-start.43 = (bf16[512]{0:T(512)(128)(2,1)S(1)}, bf16[512]{0:T(512)(128)(2,1)}, u32[]{:S(2)}) copy-start(bf16[512]{0:T(512)(128)(2,1)} %param.32) | copy-start | bytes 3076
  246.6 30.2 %copy-start.45 = (bf16[128]{0:T(256)(128)(2,1)S(1)}, bf16[128]{0:T(256)(128)(2,1)}, u32[]{:S(2)}) copy-start(bf16[128]{0:T(256)(128)(2,1)} %param.30) | copy-start | bytes 772
  246.6 38.6 %copy-start.46 = (bf16[128]{0:T(256)(128)(2,1)S(1)}, bf16[128]{0:T(256)(128)(2,1)}, u32[]{:S(2)}) copy-start(bf16[128]{0:T(256)(128)(2,1)} %param.29) | copy-start | bytes 772
  246.6 46.7 %copy-start.38 = (s32[384]{0:T(512)S(1)}, s32[384]{0:T(512)}, u32[]{:S(2)}) copy-start(s32[384]{0:T(512)} %param.21) | copy-start | bytes 4612
  254.9 38.5 %all-to-all-start.1 = ((bf16[4,384,256]{1,2,0:T(8,128)(2,1)}), bf16[4,384,256]{1,2,0:T(8,128)(2,1)}, u32[]{:S(2)}, u32[]{:S(2)}) async-start(bf16[4,384,256]{1,2,0:T(8,128)(2,1)} %copy.85), calls=%async_computation.1 | async-start | bytes 1572864 | tf_op jit(solution)/shard_map/all_to_all | solution.py:160
  259.3 354.8 %reduce-scatter.13.cloned.1.call-start = ((), (), s32[]{:S(2)}) async-start(), calls=%async_computation.17 | async-start | bytes 2359296 | tf_op jit(solution)/shard_map/reduce_scatter | solution.py:279
  293.4 69.2 %copy-start.26 = (f32[384]{0:T(512)}, f32[384]{0:T(512)S(1)}, u32[]{:S(2)}) copy-start(f32[384]{0:T(512)S(1)} %compare_convert_fusion) | copy-start | bytes 4612
  319.1 11.8 %copy-start.12 = (f32[384,1024]{1,0:T(8,128)S(1)}, f32[384,1024]{1,0:T(8,128)}, u32[]{:S(2)}) copy-start(f32[384,1024]{1,0:T(8,128)} %copy-done.11) | copy-start | bytes 4718596
  319.1 11.8 %copy-start.48 = (bf16[1024,4096]{1,0:T(8,128)(2,1)S(1)}, bf16[1024,4096]{1,0:T(8,128)(2,1)}, u32[]{:S(2)}) copy-start(bf16[1024,4096]{1,0:T(8,128)(2,1)} %all-gather.19.cloned.1.call-done) | copy-start | bytes 25165828
  335.8 6.8 copy-start.28
  342.6 356.0 %reduce-scatter.17.cloned.1.call-start = ((), (), s32[]{:S(2)}) async-start(), calls=%async_computation.19 | async-start | bytes 9437184 | tf_op jit(solution)/shard_map/reduce_scatter | solution.py:291
  353.0 346.1 %reduce-scatter.21.cloned.1.call-start = ((), (), s32[]{:S(2)}) async-start(), calls=%async_computation.21 | async-start | bytes 9437184 | tf_op jit(solution)/shard_map/reduce_scatter | solution.py:297
  353.1 9.4 %copy-start.16 = (bf16[384,1024]{1,0:T(8,128)(2,1)S(1)}, bf16[384,1024]{1,0:T(8,128)(2,1)}, u32[]{:S(2)}) copy-start(bf16[384,1024]{1,0:T(8,128)(2,1)} %param.35) | copy-start | bytes 2359300
  353.1 9.4 %copy-start.52 = (bf16[384,4096]{1,0:T(8,128)(2,1)S(1)}, bf16[384,4096]{1,0:T(8,128)(2,1)}, u32[]{:S(2)}) copy-start(bf16[384,4096]{1,0:T(8,128)(2,1)} %get-tuple-element.226) | copy-start | bytes 9437188
  358.1 11.5 %collective-permute-start = (bf16[384,256]{1,0:T(8,128)(2,1)}, bf16[384,256]{1,0:T(8,128)(2,1)S(1)}, u32[]{:S(2)}, u32[]{:S(2)}) collective-permute-start(bf16[384,256]{1,0:T(8,128)(2,1)} %get-tuple-element.238), channel_id=1, source_target_pairs={{0,1},{1,0},{2,3},{3,2},{4,5},{5,4},{6,7},{7,6},{8,9},{9,8},{10,11... | collective-permute-start | bytes 589832 | tf_op jit(solution)/shard_map/ppermute | solution.py:24
  360.1 17.3 %collective-permute-start.1 = (bf16[384,256]{1,0:T(8,128)(2,1)}, bf16[384,256]{1,0:T(8,128)(2,1)S(1)}, u32[]{:S(2)}, u32[]{:S(2)}) collective-permute-start(bf16[384,256]{1,0:T(8,128)(2,1)} %get-tuple-element.237), channel_id=1, source_target_pairs={{0,2},{1,3},{2,0},{3,1},{4,6},{5,7},{6,4},{7,5},{8,10},{9,11},{10,... | collective-permute-start | bytes 589832 | tf_op jit(solution)/shard_map/ppermute | solution.py:24
  362.4 18.0 %collective-permute-start.2 = (bf16[384,256]{1,0:T(8,128)(2,1)}, bf16[384,256]{1,0:T(8,128)(2,1)S(1)}, u32[]{:S(2)}, u32[]{:S(2)}) collective-permute-start(bf16[384,256]{1,0:T(8,128)(2,1)} %get-tuple-element.236), channel_id=1, source_target_pairs={{0,3},{1,2},{2,1},{3,0},{4,7},{5,6},{6,5},{7,4},{8,11},{9,10},{10,... | collective-permute-start | bytes 589832 | tf_op jit(solution)/shard_map/ppermute | solution.py:24
  384.9 19.7 %copy-start.1 = (bf16[2688,4,64]{0,2,1:T(8,128)(2,1)}, bf16[2688,4,64]{0,2,1:T(8,128)(2,1)S(1)}, u32[]{:S(2)}) copy-start(bf16[2688,4,64]{0,2,1:T(8,128)(2,1)S(1)} %get-tuple-element.470) | copy-start | bytes 4128772 | tf_op jit(solution)/shard_map/while
  384.9 20.7 %copy-start.4 = (bf16[2688,4,64]{0,2,1:T(8,128)(2,1)}, bf16[2688,4,64]{0,2,1:T(8,128)(2,1)S(1)}, u32[]{:S(2)}) copy-start(bf16[2688,4,64]{0,2,1:T(8,128)(2,1)S(1)} %get-tuple-element.473) | copy-start | bytes 4128772 | tf_op jit(solution)/shard_map/while
  427.9 21.7 %copy-start.3 = (f32[2688,4,64]{0,2,1:T(8,128)S(1)}, f32[2688,4,64]{0,2,1:T(8,128)}, u32[]{:S(2)}) copy-start(f32[2688,4,64]{0,2,1:T(8,128)} %get-tuple-element.447) | copy-start | bytes 8257540 | tf_op jit(solution)/shard_map/while
  427.9 21.7 %copy-start.6 = (bf16[1536,4,64]{0,2,1:T(8,128)(2,1)S(1)}, bf16[1536,4,64]{0,2,1:T(8,128)(2,1)}, u32[]{:S(2)}) copy-start(bf16[1536,4,64]{0,2,1:T(8,128)(2,1)} %get-tuple-element.467) | copy-start | bytes 2359300 | tf_op jit(solution)/shard_map/while
  474.7 10.4 %copy-start.2 = (bf16[2688,4,64]{0,2,1:T(8,128)(2,1)S(1)}, bf16[2688,4,64]{0,2,1:T(8,128)(2,1)}, u32[]{:S(2)}) copy-start(bf16[2688,4,64]{0,2,1:T(8,128)(2,1)} %copy-done.1) | copy-start | bytes 4128772 | tf_op jit(solution)/shard_map/while
  485.1 9.6 %copy-start.5 = (bf16[2688,4,64]{0,2,1:T(8,128)(2,1)S(1)}, bf16[2688,4,64]{0,2,1:T(8,128)(2,1)}, u32[]{:S(2)}) copy-start(bf16[2688,4,64]{0,2,1:T(8,128)(2,1)} %copy-done.4) | copy-start | bytes 4128772 | tf_op jit(solution)/shard_map/while
  494.7 16.4 %copy-start.1 = (bf16[2688,4,64]{0,2,1:T(8,128)(2,1)}, bf16[2688,4,64]{0,2,1:T(8,128)(2,1)S(1)}, u32[]{:S(2)}) copy-start(bf16[2688,4,64]{0,2,1:T(8,128)(2,1)S(1)} %get-tuple-element.470) | copy-start | bytes 4128772 | tf_op jit(solution)/shard_map/while
  494.7 17.4 %copy-start.4 = (bf16[2688,4,64]{0,2,1:T(8,128)(2,1)}, bf16[2688,4,64]{0,2,1:T(8,128)(2,1)S(1)}, u32[]{:S(2)}) copy-start(bf16[2688,4,64]{0,2,1:T(8,128)(2,1)S(1)} %get-tuple-element.473) | copy-start | bytes 4128772 | tf_op jit(solution)/shard_map/while
  534.3 21.3 %copy-start.3 = (f32[2688,4,64]{0,2,1:T(8,128)S(1)}, f32[2688,4,64]{0,2,1:T(8,128)}, u32[]{:S(2)}) copy-start(f32[2688,4,64]{0,2,1:T(8,128)} %get-tuple-element.447) | copy-start | bytes 8257540 | tf_op jit(solution)/shard_map/while
  534.3 21.3 %copy-start.6 = (bf16[1536,4,64]{0,2,1:T(8,128)(2,1)S(1)}, bf16[1536,4,64]{0,2,1:T(8,128)(2,1)}, u32[]{:S(2)}) copy-start(bf16[1536,4,64]{0,2,1:T(8,128)(2,1)} %get-tuple-element.467) | copy-start | bytes 2359300 | tf_op jit(solution)/shard_map/while
  579.5 9.5 %copy-start.2 = (bf16[2688,4,64]{0,2,1:T(8,128)(2,1)S(1)}, bf16[2688,4,64]{0,2,1:T(8,128)(2,1)}, u32[]{:S(2)}) copy-start(bf16[2688,4,64]{0,2,1:T(8,128)(2,1)} %copy-done.1) | copy-start | bytes 4128772 | tf_op jit(solution)/shard_map/while
  589.0 8.9 %copy-start.5 = (bf16[2688,4,64]{0,2,1:T(8,128)(2,1)S(1)}, bf16[2688,4,64]{0,2,1:T(8,128)(2,1)}, u32[]{:S(2)}) copy-start(bf16[2688,4,64]{0,2,1:T(8,128)(2,1)} %copy-done.4) | copy-start | bytes 4128772 | tf_op jit(solution)/shard_map/while
  598.1 4.5 copy-start.18
  610.0 77.6 %all-to-all-start.2 = ((bf16[1536,3,256]{2,1,0:T(4,128)(2,1)}), bf16[1536,3,256]{2,1,0:T(4,128)(2,1)S(1)}, u32[]{:S(2)}, u32[]{:S(2)}) async-start(bf16[1536,3,256]{2,1,0:T(4,128)(2,1)} %copy.89), calls=%async_computation.2 | async-start | bytes 6291456 | tf_op jit(solution)/shard_map/all_to_all | solution.py:251
  614.2 106.4 %reduce-scatter.15.cloned.1.call-start = ((), (), s32[]{:S(2)}) async-start(), calls=%async_computation.18 | async-start | bytes 327680 | tf_op jit(solution)/shard_map/reduce_scatter | solution.py:320
  614.9 143.0 %reduce-scatter.9.cloned.1.call-start = ((), (), s32[]{:S(2)}) async-start(), calls=%async_computation.15 | async-start | bytes 7077888 | tf_op jit(solution)/shard_map/reduce_scatter | solution.py:270
  692.5 5.9 copy-start.14
  698.4 9.6 %copy-start.50 = (u32[32]{0:T(128)S(1)}, u32[32]{0:T(128)}, u32[]{:S(2)}) copy-start(u32[32]{0:T(128)} %constant.167) | copy-start | bytes 388
  698.4 10.2 %copy-start.49 = (u32[32]{0:T(128)S(1)}, u32[32]{0:T(128)}, u32[]{:S(2)}) copy-start(u32[32]{0:T(128)} %constant.171) | copy-start | bytes 388
  698.4 13.4 %copy-start.13 = (f32[384,1024]{1,0:T(8,128)S(1)}, f32[384,1024]{1,0:T(8,128)}, u32[]{:S(2)}) copy-start(f32[384,1024]{1,0:T(8,128)} %copy-done.11) | copy-start | bytes 4718596
  698.5 13.4 %copy-start.27 = (f32[384]{0:T(512)S(1)}, f32[384]{0:T(512)}, u32[]{:S(2)}) copy-start(f32[384]{0:T(512)} %copy-done.26) | copy-start | bytes 4612
  698.5 106.6 %reduce-scatter.19.cloned.1.call-start = ((), (), s32[]{:S(2)}) async-start(), calls=%async_computation.20 | async-start | bytes 1310720 | tf_op jit(solution)/shard_map/reduce_scatter | solution.py:332
  699.1 116.4 %reduce-scatter.23.cloned.1.call-start = ((), (), s32[]{:S(2)}) async-start(), calls=%async_computation.22 | async-start | bytes 1310720 | tf_op jit(solution)/shard_map/reduce_scatter | solution.py:338
  699.8 139.8 %reduce-scatter.11.cloned.1.call-start = ((), (), s32[]{:S(2)}) async-start(), calls=%async_computation.16 | async-start | bytes 983040 | tf_op jit(solution)/shard_map/reduce_scatter | solution.py:311
  722.1 7.5 copy-start.31
  729.5 32.3 %copy-start.34 = (bf16[1024]{0:T(1024)(128)(2,1)S(1)}, bf16[1024]{0:T(1024)(128)(2,1)}, u32[]{:S(2)}) copy-start(bf16[1024]{0:T(1024)(128)(2,1)} %get-tuple-element.222) | copy-start | bytes 6148
  729.5 32.3 %copy-start.35 = (bf16[1024]{0:T(1024)(128)(2,1)S(1)}, bf16[1024]{0:T(1024)(128)(2,1)}, u32[]{:S(2)}) copy-start(bf16[1024]{0:T(1024)(128)(2,1)} %get-tuple-element.235) | copy-start | bytes 6148
  729.5 32.3 %copy-start.36 = (bf16[4096]{0:T(1024)(128)(2,1)S(1)}, bf16[4096]{0:T(1024)(128)(2,1)}, u32[]{:S(2)}) copy-start(bf16[4096]{0:T(1024)(128)(2,1)} %get-tuple-element.245) | copy-start | bytes 24580
  729.5 32.3 %copy-start.41 = (bf16[1024]{0:T(1024)(128)(2,1)S(1)}, bf16[1024]{0:T(1024)(128)(2,1)}, u32[]{:S(2)}) copy-start(bf16[1024]{0:T(1024)(128)(2,1)} %get-tuple-element.153) | copy-start | bytes 6148
  729.5 32.3 %copy-start.42 = (bf16[1024]{0:T(1024)(128)(2,1)S(1)}, bf16[1024]{0:T(1024)(128)(2,1)}, u32[]{:S(2)}) copy-start(bf16[1024]{0:T(1024)(128)(2,1)} %get-tuple-element.159) | copy-start | bytes 6148
  729.5 72.2 %copy-start.10 = (f32[384,1024]{1,0:T(8,128)S(1)}, f32[384,1024]{1,0:T(8,128)}, u32[]{:S(2)}) copy-start(f32[384,1024]{1,0:T(8,128)} %copy-done.9) | copy-start | bytes 4718596
  729.5 72.2 %copy-start.17 = (bf16[384,1024]{1,0:T(8,128)(2,1)S(1)}, bf16[384,1024]{1,0:T(8,128)(2,1)}, u32[]{:S(2)}) copy-start(bf16[384,1024]{1,0:T(8,128)(2,1)} %param.35) | copy-start | bytes 2359300
  729.5 72.2 %copy-start.29 = (f32[384]{0:T(512)S(1)}, f32[384]{0:T(512)}, u32[]{:S(2)}) copy-start(f32[384]{0:T(512)} %copy-done.28) | copy-start | bytes 4612
  (16 other events, 37.2 us)
Sparse Core Ops, SparseCore 0:
  9.9 48.2 all-gather.14
  60.1 27.8 all-gather.16
  89.9 54.3 all-gather.18
  146.1 54.3 all-gather.20
  342.7 41.5 reduce-scatter.12
  388.0 71.2 reduce-scatter.16
  462.8 71.2 reduce-scatter.20
  617.3 25.4 reduce-scatter.14
  698.6 59.2 reduce-scatter.8
  760.1 27.1 reduce-scatter.18
  789.6 25.8 reduce-scatter.22
  817.8 21.8 reduce-scatter.10
